TPU v7x, 1024 devices: a whole 4x8x16 slice. The times are simulated.
1024 devices in a mesh: rows: 128 (over z, y), cols: 8 (over x, core).
Axes of the slice: x: 4, y: 8, z: 16, core: 2. Of those that a mesh axis runs over, the one named last changes fastest.
Arguments:
- z_blocks: float32 [512, 8, 256, 256], P('rows', 'cols'), may hold values from -0.125 to 0.125
- z_cols: int32 [512, 8], P('rows', 'cols'), may hold values from 0 to 511, as said below
- z_count: int32 [512], P('rows'), may hold values from 2 to 8, as said below
- h_blocks: float32 [512, 8, 256, 256], P('rows', 'cols'), may hold values from -0.125 to 0.125
- h_cols: int32 [512, 8], P('rows', 'cols'), may hold values from 0 to 511, as said below
- h_count: int32 [512], P('rows'), may hold values from 2 to 8, as said below
- panel: float32 [512, 256, 64], P('rows'), may hold values from -6 to 6
Outputs:
- result: float32 [512, 256, 64], P('rows', 'cols')
Inputs may be any that keep to these rules, and one draw needn't show every extreme that they name: `z_cols`: within a block row the column block indices of the slots are distinct; block row i only names blocks from 4 * (i // 4) - 4 to 4 * (i // 4) + 7. `h_cols`: same law as z_cols, drawn apart. `z_count`: block row 0 uses all 8 slots. `h_count`: block row 0 uses all 8 slots.
All inputs are finite; a program needn't handle non-finite values.
Results may differ from a plain program's by a relative error of at most 0.000098.
Values sent between devices are 32-bit elements; how exact they have to be, the bound alone decides.
No kernel may reach another device: no remote copies, remote signals or barrier semaphores. Data moves between devices by JAX's collectives and lax.ppermute only.
A program may use at most 32 MiB of HBM per device.

v0:
```python
import jax
import jax.numpy as jnp
from jax import lax
from jax.sharding import PartitionSpec as P

HB = 4


def with_halo(block, sides, width):
    for axis, dim in sides:
        count = lax.axis_size(axis)
        forward = [(i, i + 1) for i in range(count - 1)]
        backward = [(target, source) for source, target in forward]
        low = lax.ppermute(
            lax.slice_in_dim(block, block.shape[dim] - width, None, axis=dim), axis, forward
        )
        high = lax.ppermute(lax.slice_in_dim(block, 0, width, axis=dim), axis, backward)
        block = jnp.concatenate([low, block, high], axis=dim)
    return block


def in_blocks(x, dim, devices):
    lengths = x.shape
    parts = x.reshape(*lengths[:dim], devices, lengths[dim] // devices, *lengths[dim + 1 :])
    return jnp.moveaxis(parts, dim, 0)


def sum_at_owner(x, axis, dim):
    parts = in_blocks(x, dim, lax.axis_size(axis))
    arrived = lax.all_to_all(parts, axis, split_axis=0, concat_axis=0, tiled=True)
    return arrived.sum(axis=0)


def copy_for_each(x, axis):
    devices = lax.axis_size(axis)
    return lax.all_to_all(jnp.broadcast_to(x[None], (devices, *x.shape)), axis, 0, 0, tiled=True)


def of_everyone(x, axis):
    everything = copy_for_each(x, axis)
    return jnp.sum(everything, axis=0)


def slot_mask(count, slots):
    first = lax.axis_index("cols") * slots
    return (first + jnp.arange(slots)[None, :] < count[:, None]).astype(jnp.float32)


def window_start(own_rows):
    return lax.axis_index("rows") * own_rows - HB


def whole_window(field):
    return with_halo(field, (("rows", 0),), HB)


def contract(blocks, cols, count, window, own_rows):
    offsets = cols - window_start(own_rows)
    picked = window[offsets] * slot_mask(count, cols.shape[1])[:, :, None, None]
    return jnp.einsum("aspq,asqn->apn", blocks, picked, precision=lax.Precision.HIGHEST)


def return_rims(buffer, own_rows):
    rims = jnp.concatenate([buffer[:HB], buffer[HB + own_rows :]], axis=0)
    arrived = with_halo(rims, (("rows", 0),), HB)
    from_below = arrived[:HB]
    from_above = arrived[3 * HB :]
    owned = buffer[HB : HB + own_rows]
    owned = owned.at[:HB].add(from_below)
    owned = owned.at[own_rows - HB :].add(from_above)
    return owned


def owner_fold(values):
    return sum_at_owner(values, "cols", 1)


def local(z_blocks, z_cols, z_count, h_blocks, h_cols, h_count, panel):
    own_rows = panel.shape[0]
    mid_part = contract(z_blocks, z_cols, z_count, whole_window(panel), own_rows)
    mid = of_everyone(mid_part, "cols")
    side_part = contract(h_blocks, h_cols, h_count, whole_window(mid), own_rows)
    side = of_everyone(side_part, "cols")
    mask = slot_mask(z_count, z_cols.shape[1])
    terms = jnp.einsum("asqp,aqn->aspn", z_blocks, side, precision=lax.Precision.HIGHEST)
    offsets = z_cols - window_start(own_rows)
    spread = own_rows + 2 * HB
    placing = (offsets[:, :, None] == jnp.arange(spread)[None, None, :]).astype(jnp.float32)
    placing = placing * mask[:, :, None]
    buffer = jnp.einsum("asw,aspn->wpn", placing, terms, precision=lax.Precision.HIGHEST)
    owned = return_rims(buffer, own_rows)
    result = owner_fold(owned)
    return result


def solution(mesh):
    return jax.shard_map(
        local,
        mesh=mesh,
        in_specs=(
            P("rows", "cols", None, None),
            P("rows", "cols"),
            P("rows"),
            P("rows", "cols", None, None),
            P("rows", "cols"),
            P("rows"),
            P("rows", None, None),
        ),
        out_specs=P("rows", "cols", None),
        check_vma=False,
    )
```

profile of v0, /device:TPU:248, one launch (start us, length us, event | category | flops | bytes accessed | tf_op | source)
XLA Modules:
  0.0 131.2 jit_solution(17607048352559230531)
XLA Ops:
  0.0 0.0 copy-start
  0.0 4.8 %collective-permute-start = (f32[4,256,64]{1,2,0:T(8,128)}, f32[4,256,64]{1,2,0:T(8,128)S(1)}, u32[]{:S(2)}, u32[]{:S(2)}) collective-permute-start(f32[4,256,64]{1,2,0:T(8,128)} %param.21), channel_id=1, source_target_pairs={{0,8},{8,16},{16,24},{24,32},{32,40},{40,48},{48,56},{56,64},{64,7... | collective-permute-start | bytes 786440 | tf_op jit(solution)/shard_map/ppermute | solution.py:14
  4.8 1.9 %collective-permute-start.1 = (f32[4,256,64]{1,2,0:T(8,128)}, f32[4,256,64]{1,2,0:T(8,128)S(1)}, u32[]{:S(2)}, u32[]{:S(2)}) collective-permute-start(f32[4,256,64]{1,2,0:T(8,128)} %param.21), channel_id=1, source_target_pairs={{8,0},{16,8},{24,16},{32,24},{40,32},{48,40},{56,48},{64,56},{72,6... | collective-permute-start | bytes 786440 | tf_op jit(solution)/shard_map/ppermute | solution.py:17
  6.8 0.7 subtract_bitcast_fusion
  7.4 0.7 compare_convert_fusion.1
  8.1 2.6 %collective-permute-done = f32[4,256,64]{1,2,0:T(8,128)S(1)} collective-permute-done((f32[4,256,64]{1,2,0:T(8,128)}, f32[4,256,64]{1,2,0:T(8,128)S(1)}, u32[]{:S(2)}, u32[]{:S(2)}) %collective-permute-start) | collective-permute-done | bytes 262176 | tf_op jit(solution)/shard_map/ppermute | solution.py:14
  10.7 7.3 %collective-permute-done.1 = f32[4,256,64]{1,2,0:T(8,128)S(1)} collective-permute-done((f32[4,256,64]{1,2,0:T(8,128)}, f32[4,256,64]{1,2,0:T(8,128)S(1)}, u32[]{:S(2)}, u32[]{:S(2)}) %collective-permute-start.1) | collective-permute-done | bytes 262176 | tf_op jit(solution)/shard_map/ppermute | solution.py:17
  18.0 1.0 pad_maximum_fusion
  19.0 0.6 gather_fusion
  19.6 0.0 copy-done
  19.6 1.1 convolution_bitcast_fusion.2
  20.8 1.6 %broadcast_in_dim.9 = f32[8,4,256,64]{2,3,1,0:T(8,128)} broadcast(f32[4,256,64]{1,2,0:T(8,128)S(1)} %convolution_bitcast_fusion.2), dimensions={1,2,3} | broadcast | bytes 2359296 | tf_op jit(solution)/shard_map/broadcast_in_dim | solution.py:36
  22.3 0.0 copy-start.2
  22.3 4.4 %all-to-all-start = ((f32[8,4,256,64]{2,3,1,0:T(8,128)}), f32[8,4,256,64]{2,3,1,0:T(8,128)S(1)}, u32[]{:S(2)}, u32[]{:S(2)}) async-start(f32[8,4,256,64]{2,3,1,0:T(8,128)} %broadcast_in_dim.9), calls=%async_computation | async-start | bytes 4194304 | tf_op jit(solution)/shard_map/all_to_all | solution.py:36
  26.8 0.0 copy-done.2
  26.8 0.0 copy-start.3
  26.8 27.1 %all-to-all-done = f32[8,4,256,64]{2,3,1,0:T(8,128)S(1)} async-done(((f32[8,4,256,64]{2,3,1,0:T(8,128)}), f32[8,4,256,64]{2,3,1,0:T(8,128)S(1)}, u32[]{:S(2)}, u32[]{:S(2)}) %all-to-all-start) | async-done | bytes 2097184 | tf_op jit(solution)/shard_map/all_to_all | solution.py:36
  53.9 0.1 reduce_sum.27
  54.1 0.0 copy-start.1
  54.1 2.1 %collective-permute-start.2 = (f32[4,256,64]{1,2,0:T(8,128)S(1)}, f32[4,256,64]{1,2,0:T(8,128)S(1)}, u32[]{:S(2)}, u32[]{:S(2)}) collective-permute-start(f32[4,256,64]{1,2,0:T(8,128)S(1)} %reduce_sum.27), channel_id=1, source_target_pairs={{0,8},{8,16},{16,24},{24,32},{32,40},{40,48},{48,56},{56,64},{64,7... | collective-permute-start | bytes 786440 | tf_op jit(solution)/shard_map/ppermute | solution.py:14
  56.2 3.9 %collective-permute-start.3 = (f32[4,256,64]{1,2,0:T(8,128)S(1)}, f32[4,256,64]{1,2,0:T(8,128)S(1)}, u32[]{:S(2)}, u32[]{:S(2)}) collective-permute-start(f32[4,256,64]{1,2,0:T(8,128)S(1)} %reduce_sum.27), channel_id=1, source_target_pairs={{8,0},{16,8},{24,16},{32,24},{40,32},{48,40},{56,48},{64,56},{72,6... | collective-permute-start | bytes 786440 | tf_op jit(solution)/shard_map/ppermute | solution.py:17
  60.1 0.0 copy-done.3
  60.1 3.7 %collective-permute-done.2 = f32[4,256,64]{1,2,0:T(8,128)S(1)} collective-permute-done((f32[4,256,64]{1,2,0:T(8,128)S(1)}, f32[4,256,64]{1,2,0:T(8,128)S(1)}, u32[]{:S(2)}, u32[]{:S(2)}) %collective-permute-start.2) | collective-permute-done | bytes 262176 | tf_op jit(solution)/shard_map/ppermute | solution.py:14
  63.9 5.2 %collective-permute-done.3 = f32[4,256,64]{1,2,0:T(8,128)S(1)} collective-permute-done((f32[4,256,64]{1,2,0:T(8,128)S(1)}, f32[4,256,64]{1,2,0:T(8,128)S(1)}, u32[]{:S(2)}, u32[]{:S(2)}) %collective-permute-start.3) | collective-permute-done | bytes 262176 | tf_op jit(solution)/shard_map/ppermute | solution.py:17
  69.1 0.1 pad_maximum_fusion.1
  69.2 0.6 gather_fusion.1
  69.8 0.0 copy-done.1
  69.8 1.1 convolution_bitcast_fusion.1
  70.9 0.2 broadcast_in_dim.11
  71.2 29.7 %all_to_all.15 = f32[8,4,256,64]{2,3,1,0:T(8,128)S(1)} all-to-all(f32[8,4,256,64]{2,3,1,0:T(8,128)S(1)} %broadcast_in_dim.11), channel_id=1, replica_groups=mesh['rows'=128,'cols'=8] {'cols'}, dimensions={0} | all-to-all | bytes 4194304 | tf_op jit(solution)/shard_map/all_to_all | solution.py:36
  100.8 0.1 reduce_sum.28
  101.0 0.8 convolution_bitcast_fusion
  101.7 1.2 fusion.4
  103.0 0.1 fusion.18
  103.0 1.9 %collective-permute-start.4 = (f32[4,256,64]{1,0,2:T(4,128)S(1)}, f32[4,256,64]{1,0,2:T(4,128)S(1)}, u32[]{:S(2)}, u32[]{:S(2)}) collective-permute-start(f32[4,256,64]{1,0,2:T(4,128)S(1)} %get-tuple-element.45), channel_id=1, source_target_pairs={{0,8},{8,16},{16,24},{24,32},{32,40},{40,48},{48,56},{56,64},{64,7... | collective-permute-start | bytes 786440 | tf_op jit(solution)/shard_map/ppermute | solution.py:14
  105.0 3.9 %collective-permute-start.5 = (f32[4,256,64]{1,0,2:T(4,128)S(1)}, f32[4,256,64]{1,0,2:T(4,128)S(1)}, u32[]{:S(2)}, u32[]{:S(2)}) collective-permute-start(f32[4,256,64]{1,0,2:T(4,128)S(1)} %get-tuple-element.46), channel_id=1, source_target_pairs={{8,0},{16,8},{24,16},{32,24},{40,32},{48,40},{56,48},{64,56},{72,6... | collective-permute-start | bytes 786440 | tf_op jit(solution)/shard_map/ppermute | solution.py:17
  108.9 3.7 %collective-permute-done.4 = f32[4,256,64]{1,0,2:T(4,128)S(1)} collective-permute-done((f32[4,256,64]{1,0,2:T(4,128)S(1)}, f32[4,256,64]{1,0,2:T(4,128)S(1)}, u32[]{:S(2)}, u32[]{:S(2)}) %collective-permute-start.4) | collective-permute-done | bytes 262176 | tf_op jit(solution)/shard_map/ppermute | solution.py:14
  112.6 5.2 %collective-permute-done.5 = f32[4,256,64]{1,0,2:T(4,128)S(1)} collective-permute-done((f32[4,256,64]{1,0,2:T(4,128)S(1)}, f32[4,256,64]{1,0,2:T(4,128)S(1)}, u32[]{:S(2)}, u32[]{:S(2)}) %collective-permute-start.5) | collective-permute-done | bytes 262176 | tf_op jit(solution)/shard_map/ppermute | solution.py:17
  117.9 0.1 fusion.3
  118.0 0.2 copy.17
  118.3 0.3 reshape.168
  118.6 9.9 %all_to_all.16 = f32[8,1,8192]{2,1,0:T(1,128)S(1)} all-to-all(f32[8,1,8192]{2,1,0:T(1,128)S(1)} %reshape.168), channel_id=1, replica_groups=mesh['rows'=128,'cols'=8] {'cols'}, dimensions={0} | all-to-all | bytes 524288 | tf_op jit(solution)/shard_map/all_to_all | solution.py:30
  128.5 0.5 broadcast.143
  129.0 1.3 reduce.4
  130.3 0.2 reshape.169
  130.5 0.7 reduce_sum.29
  (5 shorter events, 0.1 us)
Async XLA Ops:
  0.0 19.6 %copy-start = (f32[4,1,256,256]{3,2,1,0:T(8,128)S(1)}, f32[4,1,256,256]{3,2,1,0:T(8,128)}, u32[]{:S(2)}) copy-start(f32[4,1,256,256]{3,2,1,0:T(8,128)} %param.15) | copy-start | bytes 3145732
  0.0 10.7 %collective-permute-start = (f32[4,256,64]{1,2,0:T(8,128)}, f32[4,256,64]{1,2,0:T(8,128)S(1)}, u32[]{:S(2)}, u32[]{:S(2)}) collective-permute-start(f32[4,256,64]{1,2,0:T(8,128)} %param.21), channel_id=1, source_target_pairs={{0,8},{8,16},{16,24},{24,32},{32,40},{40,48},{48,56},{56,64},{64,7... | collective-permute-start | bytes 786440 | tf_op jit(solution)/shard_map/ppermute | solution.py:14
  4.8 13.2 %collective-permute-start.1 = (f32[4,256,64]{1,2,0:T(8,128)}, f32[4,256,64]{1,2,0:T(8,128)S(1)}, u32[]{:S(2)}, u32[]{:S(2)}) collective-permute-start(f32[4,256,64]{1,2,0:T(8,128)} %param.21), channel_id=1, source_target_pairs={{8,0},{16,8},{24,16},{32,24},{40,32},{48,40},{56,48},{64,56},{72,6... | collective-permute-start | bytes 786440 | tf_op jit(solution)/shard_map/ppermute | solution.py:17
  22.3 4.4 %copy-start.2 = (s32[4,1]{0,1:T(1,128)S(1)}, s32[4,1]{0,1:T(1,128)}, u32[]{:S(2)}) copy-start(s32[4,1]{0,1:T(1,128)} %param.19) | copy-start | bytes 52
  22.3 31.6 %all-to-all-start = ((f32[8,4,256,64]{2,3,1,0:T(8,128)}), f32[8,4,256,64]{2,3,1,0:T(8,128)S(1)}, u32[]{:S(2)}, u32[]{:S(2)}) async-start(f32[8,4,256,64]{2,3,1,0:T(8,128)} %broadcast_in_dim.9), calls=%async_computation | async-start | bytes 4194304 | tf_op jit(solution)/shard_map/all_to_all | solution.py:36
  26.8 33.3 %copy-start.3 = (s32[4]{0:T(128)S(1)}, s32[4]{0:T(128)}, u32[]{:S(2)}) copy-start(s32[4]{0:T(128)} %param.20) | copy-start | bytes 52
  54.1 15.7 %copy-start.1 = (f32[4,1,256,256]{3,2,1,0:T(8,128)S(1)}, f32[4,1,256,256]{3,2,1,0:T(8,128)}, u32[]{:S(2)}) copy-start(f32[4,1,256,256]{3,2,1,0:T(8,128)} %param.18) | copy-start | bytes 3145732
  54.1 9.8 %collective-permute-start.2 = (f32[4,256,64]{1,2,0:T(8,128)S(1)}, f32[4,256,64]{1,2,0:T(8,128)S(1)}, u32[]{:S(2)}, u32[]{:S(2)}) collective-permute-start(f32[4,256,64]{1,2,0:T(8,128)S(1)} %reduce_sum.27), channel_id=1, source_target_pairs={{0,8},{8,16},{16,24},{24,32},{32,40},{40,48},{48,56},{56,64},{64,7... | collective-permute-start | bytes 786440 | tf_op jit(solution)/shard_map/ppermute | solution.py:14
  56.2 13.0 %collective-permute-start.3 = (f32[4,256,64]{1,2,0:T(8,128)S(1)}, f32[4,256,64]{1,2,0:T(8,128)S(1)}, u32[]{:S(2)}, u32[]{:S(2)}) collective-permute-start(f32[4,256,64]{1,2,0:T(8,128)S(1)} %reduce_sum.27), channel_id=1, source_target_pairs={{8,0},{16,8},{24,16},{32,24},{40,32},{48,40},{56,48},{64,56},{72,6... | collective-permute-start | bytes 786440 | tf_op jit(solution)/shard_map/ppermute | solution.py:17
  103.0 9.6 %collective-permute-start.4 = (f32[4,256,64]{1,0,2:T(4,128)S(1)}, f32[4,256,64]{1,0,2:T(4,128)S(1)}, u32[]{:S(2)}, u32[]{:S(2)}) collective-permute-start(f32[4,256,64]{1,0,2:T(4,128)S(1)} %get-tuple-element.45), channel_id=1, source_target_pairs={{0,8},{8,16},{16,24},{24,32},{32,40},{40,48},{48,56},{56,64},{64,7... | collective-permute-start | bytes 786440 | tf_op jit(solution)/shard_map/ppermute | solution.py:14
  105.0 12.9 %collective-permute-start.5 = (f32[4,256,64]{1,0,2:T(4,128)S(1)}, f32[4,256,64]{1,0,2:T(4,128)S(1)}, u32[]{:S(2)}, u32[]{:S(2)}) collective-permute-start(f32[4,256,64]{1,0,2:T(4,128)S(1)} %get-tuple-element.46), channel_id=1, source_target_pairs={{8,0},{16,8},{24,16},{32,24},{40,32},{48,40},{56,48},{64,56},{72,6... | collective-permute-start | bytes 786440 | tf_op jit(solution)/shard_map/ppermute | solution.py:17
where the time goes:
time: 132 us; the launch traced here: 131 us
  waiting for transfers between devices  55 us (42%)
  blocking collectives  39.6 us (30%)
  starting transfers between devices  23 us (17%)
  other arithmetic  4.78 us (4%)
  local copies, waits for them, and re-layouts  4.33 us (3%)
  matrix products  4.27 us (3%)
    all_to_all x1, blocking collectives, copy_for_each(): lax.all_to_all(jnp.broadcast_to(x[None], (devices, *x.shape)), axis, 0, 0...  29.7 us
    all_to_all x1, waiting for transfers between devices, copy_for_each(): lax.all_to_all(jnp.broadcast_to(x[None], (devices, *x.shape)), axis, 0, 0...  27.1 us
    ppermute x3, waiting for transfers between devices, with_halo(): lax.ppermute(lax.slice_in_dim(block, 0, width, axis=dim), axis, backward)  17.8 us
    ppermute x3, waiting for transfers between devices, with_halo(): lax.ppermute(lax.slice_in_dim(block, block.shape[dim] - width, None, axis...  10.1 us
    all_to_all x1, blocking collectives, sum_at_owner(): lax.all_to_all(parts, axis, split_axis=0, concat_axis=0, tiled=True)  9.91 us
    ppermute x3, starting transfers between devices, with_halo(): lax.ppermute(lax.slice_in_dim(block, 0, width, axis=dim), axis, backward)  9.77 us
    ppermute x3, starting transfers between devices, with_halo(): lax.ppermute(lax.slice_in_dim(block, block.shape[dim] - width, None, axis...  8.79 us
    all_to_all x1, starting transfers between devices, copy_for_each(): lax.all_to_all(jnp.broadcast_to(x[None], (devices, *x.shape)), axis, 0, 0...  4.43 us
  transfers between devices with their start and end apart: 7, of which 7 were waited for; matrix products, arithmetic and copies ran while one was open for 1% of the time, Pallas kernels for 0%

commit v1 on v0

v1 whole, which is shorter than its diff:
```python
import jax
import jax.numpy as jnp
from jax import lax
from jax.experimental import pallas as pl
from jax.experimental.pallas import tpu as pltpu
from jax.sharding import Mesh, PartitionSpec as P


HB = 4
VMEM = pl.BlockSpec(memory_space=pltpu.VMEM)


def split(x):
    high = x.astype(jnp.bfloat16)
    low = (x - high.astype(jnp.float32)).astype(jnp.bfloat16)
    return high, low


def product(x, block, dims):
    m = x.shape[0]
    xh, xl = split(x)
    bh, bl = split(block)
    dot = lambda a, b: lax.dot_general(a, b, (dims, ((), ())), preferred_element_type=jnp.float32)
    both = dot(jnp.concatenate([xh, xl], axis=0), bh)
    return both[:m] + (both[m:] + dot(xh, bl))


def pick(fields, index):
    picked = jnp.zeros(fields[0].shape, jnp.float32)
    for w, field in enumerate(fields):
        picked = jnp.where(index == w, field, picked)
    return picked


def forward_kernel(row, low, own, high, mine, theirs, index_mine, index_theirs, out):
    n = own.shape[1]
    fields = [ref[j] for ref in (low, own, high) for j in range(HB)]
    for i in range(HB):
        total = None
        for blocks, index in ((mine, index_mine), (theirs, index_theirs)):
            where = jnp.broadcast_to(index[pl.ds(index.shape[0] - 8 + row + i, 1), :], (n, 256))
            part = product(pick(fields, where), blocks[pl.ds(i * 256, 256), :], ((1,), (1,)))
            total = part if total is None else total + part
        for x in range(out.shape[0]):
            out[x, i] = total


def backward_kernel(parts, mine, theirs, index_mine, index_theirs, low, own, high):
    n = own.shape[1]
    outs = [(ref, j) for ref in (low, own, high) for j in range(HB)]
    for ref, j in outs:
        ref[j] = jnp.zeros((n, 256), jnp.float32)
    for i in range(HB):
        side = (parts[0, i] + parts[1, i]) + (parts[2, i] + parts[3, i])
        for blocks, index in ((mine, index_mine), (theirs, index_theirs)):
            where = jnp.broadcast_to(index[pl.ds(index.shape[0] - 8 + i, 1), :], (n, 256))
            term = product(side, blocks[pl.ds(i * 256, 256), :], ((1,), (0,)))
            for w, (ref, j) in enumerate(outs):
                ref[j] = ref[j] + jnp.where(where == w, term, 0.0)


def pack_kernel(own, below, above, out):
    for t in range(2):
        for j in range(HB):
            total = (
                own[j, :, pl.ds(128 * t, 128)]
                + below[j, :, pl.ds(128 * t, 128)]
                + above[j, :, pl.ds(128 * t, 128)]
            )
            for u in range(4):
                shift = (32 * (j - u)) % 128
                turned = total if shift == 0 else pltpu.roll(total, shift, 1)
                out[4 * t + u, :, pl.ds(32 * j, 32)] = turned[:, 32 * j : 32 * j + 32]


def final_kernel(parts, out):
    halves = []
    for q in range(2):
        halves.append((parts[q] + parts[2 + q]) + (parts[4 + q] + parts[6 + q]))
    total = jnp.concatenate(halves + halves, axis=0)
    out[...] = jnp.transpose(total)[:, :64].reshape(out.shape)


def call(kernel, out_shape, count, flops, size):
    return pl.pallas_call(
        kernel,
        out_shape=out_shape,
        in_specs=[VMEM] * count,
        out_specs=jax.tree.map(lambda _: VMEM, out_shape),
        cost_estimate=pl.CostEstimate(flops=flops, bytes_accessed=size, transcendentals=0),
        compiler_params=pltpu.CompilerParams(vmem_limit_bytes=8 << 20),
    )


def f32(*shape):
    return jax.ShapeDtypeStruct(shape, jnp.float32)


def neighbours(up, down):
    count = lax.axis_size("rows")
    below = lax.ppermute(up, "rows", [(i, i + 1) for i in range(count - 1)])
    above = lax.ppermute(down, "rows", [(i + 1, i) for i in range(count - 1)])
    return below, above


def steps(z_blocks, z_cols, z_count, h_blocks, h_cols, h_count, panel):
    q = lax.axis_index("core")
    slot = lax.axis_index("x") * 2 + q
    start = lax.axis_index("rows") * HB - HB
    z = z_blocks.reshape(1024, 256)
    h = h_blocks.reshape(1024, 256)

    def index_rows(cols, count):
        return jnp.where(slot < count, cols[:, 0] - start, -1)

    index = jnp.concatenate([index_rows(z_cols, z_count), index_rows(h_cols, h_count)])
    index = jnp.broadcast_to(index.astype(jnp.float32)[:, None], (8, 256))

    swap = [(0, 1), (1, 0)]
    x = lax.dynamic_slice_in_dim(jnp.swapaxes(panel, 1, 2), q * 32, 32, axis=1)
    x_low, x_high = neighbours(x, x)
    theirs = lax.ppermute(jnp.concatenate([z, index], axis=0), "core", swap)
    h_theirs = lax.ppermute(h, "core", swap)

    def forward(row, low, own, high, mine, other):
        body = lambda *refs: forward_kernel(row, *refs)
        return call(body, f32(4, HB, 32, 256), 7, 1 << 28, 1 << 22)(low, own, high, mine, other, index, theirs)

    def exchange(parts):
        return lax.all_to_all(parts, "x", 0, 0, tiled=True)

    mid = exchange(forward(0, x_low, x, x_high, z, theirs)).sum(axis=0)
    mid_low, mid_high = neighbours(mid, mid)
    side = exchange(forward(4, mid_low, mid, mid_high, h, h_theirs))
    shape = f32(HB, 32, 256)
    low, own, high = call(backward_kernel, (shape, shape, shape), 5, 1 << 28, 1 << 22)(
        side, z, theirs, index, theirs
    )
    from_below, from_above = neighbours(high, low)
    packed = call(pack_kernel, f32(8, 32, 128), 3, 1 << 20, 1 << 20)(own, from_below, from_above)
    arrived = lax.all_to_all(packed, ("x", "core"), 0, 0, tiled=True)
    return call(final_kernel, f32(HB, 32, 64), 1, 1 << 20, 1 << 18)(arrived)


def solution(mesh):
    grid = Mesh(mesh.devices.reshape(mesh.shape["rows"], 4, 2), ("rows", "x", "core"))
    cols = ("x", "core")
    return jax.shard_map(
        steps,
        mesh=grid,
        in_specs=(
            P("rows", cols, None, None),
            P("rows", cols),
            P("rows"),
            P("rows", cols, None, None),
            P("rows", cols),
            P("rows"),
            P("rows", None, None),
        ),
        out_specs=P("rows", cols, None),
        check_vma=False,
    )
```

time: 132 us -> 84.7 us (0.64)
  the two profiles are of different devices: /device:TPU:248 before, /device:TPU:504 now
where the time goes in v1:
time: 84.7 us; the launch traced here: 84.2 us
  blocking collectives  31.7 us (37%)
  starting transfers between devices  22.6 us (27%)
  waiting for transfers between devices  20.9 us (25%)
  Pallas kernels  4.41 us (5%)
  other arithmetic  4.37 us (5%)
    all_to_all x2, blocking collectives, exchange(): return lax.all_to_all(parts, 'x', 0, 0, tiled=True)  23.2 us
    ppermute x3, waiting for transfers between devices, neighbours(): above = lax.ppermute(down, 'rows', [(i + 1, i) for i in range(count - 1)])  17.9 us
    ppermute x3, starting transfers between devices, neighbours(): above = lax.ppermute(down, 'rows', [(i + 1, i) for i in range(count - 1)])  9.76 us
    ppermute x3, starting transfers between devices, neighbours(): below = lax.ppermute(up, 'rows', [(i, i + 1) for i in range(count - 1)])  8.54 us
    all_to_all x1, blocking collectives, steps(): arrived = lax.all_to_all(packed, ('x', 'core'), 0, 0, tiled=True)  8.49 us
    ppermute x3, waiting for transfers between devices, neighbours(): below = lax.ppermute(up, 'rows', [(i, i + 1) for i in range(count - 1)])  2.98 us
    pallas_call x2, Pallas kernels, forward(): call(body, f32(4, HB, 32, 256), 7, 1 << 28, 1 << 22)  2.78 us
    concatenate x1, other arithmetic, steps(): theirs = lax.ppermute(jnp.concatenate([z, index], axis=0), 'core', swap)  2.46 us
  transfers between devices with their start and end apart: 8, of which 6 were waited for; matrix products, arithmetic and copies ran while one was open for 1% of the time, Pallas kernels for 1%

profile of v1, /device:TPU:504, one launch (start us, length us, event | category | flops | bytes accessed | tf_op | source)
XLA Modules:
  0.0 84.2 jit_solution(5024571270527341246)
XLA Ops:
  0.0 0.0 copy-start
  0.0 0.8 compare_select_fusion
  0.8 0.1 add_convert_fusion
  0.8 0.1 broadcast_in_dim.12.refs_5_.index_mine
  0.9 0.0 copy-start.2
  0.9 0.0 copy-start.1
  0.9 2.5 %pad_maximum_fusion = f32[1032,256]{1,0:T(8,128)} fusion(f32[8,256]{1,0:T(8,128)S(1)} %broadcast_in_dim.12.refs_5_.index_mine, f32[1024,256]{1,0:T(8,128)} %bitcast.8), kind=kLoop, calls=%fused_computation | loop fusion | flops 264192 | bytes 2113536 | tf_op jit(solution)/shard_map/concatenate | solution.py:122
  3.4 1.9 %collective-permute-start.2 = (f32[1032,256]{1,0:T(8,128)}, f32[1032,256]{1,0:T(8,128)S(1)}, u32[]{:S(2)}, u32[]{:S(2)}) collective-permute-start(f32[1032,256]{1,0:T(8,128)} %pad_maximum_fusion), channel_id=1, source_target_pairs={{0,1},{1,0},{2,3},{3,2},{4,5},{5,4},{6,7},{7,6},{8,9},{9,8},{10,11... | collective-permute-start | bytes 3170312 | tf_op jit(solution)/shard_map/ppermute | solution.py:122
  5.3 0.0 copy-done.2
  5.3 2.4 %collective-permute-start.5 = (f32[1024,256]{1,0:T(8,128)S(1)}, f32[1024,256]{1,0:T(8,128)}, u32[]{:S(2)}, u32[]{:S(2)}) collective-permute-start(f32[1024,256]{1,0:T(8,128)S(1)} %bitcast.11), channel_id=1, source_target_pairs={{0,1},{1,0},{2,3},{3,2},{4,5},{5,4},{6,7},{7,6},{8,9},{9,8},{10,11... | collective-permute-start | bytes 3145736 | tf_op jit(solution)/shard_map/ppermute | solution.py:123
  7.7 0.0 copy-done
  7.7 4.7 %collective-permute-start = (f32[4,32,256]{2,1,0:T(8,128)S(1)}, f32[4,32,256]{2,1,0:T(8,128)S(1)}, u32[]{:S(2)}, u32[]{:S(2)}) collective-permute-start(f32[4,32,256]{2,1,0:T(8,128)S(1)} %dynamic-slice_bitcast_fusion.refs_1_), channel_id=1, source_target_pairs={{0,8},{8,16},{16,24},{24,32},{32,40},{40,48},{48,56},{56,64},{64,7... | collective-permute-start | bytes 393224 | tf_op jit(solution)/shard_map/ppermute | solution.py:101
  12.5 1.9 %collective-permute-start.1 = (f32[4,32,256]{2,1,0:T(8,128)S(1)}, f32[4,32,256]{2,1,0:T(8,128)S(1)}, u32[]{:S(2)}, u32[]{:S(2)}) collective-permute-start(f32[4,32,256]{2,1,0:T(8,128)S(1)} %dynamic-slice_bitcast_fusion.refs_1_), channel_id=1, source_target_pairs={{8,0},{16,8},{24,16},{32,24},{40,32},{48,40},{56,48},{64,56},{72,6... | collective-permute-start | bytes 393224 | tf_op jit(solution)/shard_map/ppermute | solution.py:102
  14.4 1.0 %collective-permute-done.refs_0_ = f32[4,32,256]{2,1,0:T(8,128)S(1)} collective-permute-done((f32[4,32,256]{2,1,0:T(8,128)S(1)}, f32[4,32,256]{2,1,0:T(8,128)S(1)}, u32[]{:S(2)}, u32[]{:S(2)}) %collective-permute-start) | collective-permute-done | bytes 131104 | tf_op jit(solution)/shard_map/ppermute | solution.py:101
  15.4 7.4 %collective-permute-done.1.refs_2_ = f32[4,32,256]{2,1,0:T(8,128)S(1)} collective-permute-done((f32[4,32,256]{2,1,0:T(8,128)S(1)}, f32[4,32,256]{2,1,0:T(8,128)S(1)}, u32[]{:S(2)}, u32[]{:S(2)}) %collective-permute-start.1) | collective-permute-done | bytes 131104 | tf_op jit(solution)/shard_map/ppermute | solution.py:102
  22.8 0.0 collective-permute-done.2.refs_4_.refs_6_.theirs.index_theirs
  22.8 0.0 copy-done.1
  22.8 0.8 shard_map.73
  23.6 12.7 %all_to_all.15 = f32[4,4,32,256]{3,2,1,0:T(8,128)} all-to-all(f32[4,4,32,256]{3,2,1,0:T(8,128)S(1)} %shard_map.73), channel_id=1, replica_groups=mesh['rows'=128,'x'=4,'core'=2] {'x'}, dimensions={0} | all-to-all | bytes 1048576 | tf_op jit(solution)/shard_map/all_to_all | solution.py:130
  36.3 1.1 %reduce_sum.9.refs_1_ = f32[4,32,256]{2,1,0:T(8,128)S(1)} reduce(f32[4,4,32,256]{3,2,1,0:T(8,128)} %all_to_all.15, f32[]{:T(128)} %constant.28.clone.1), dimensions={0}, to_apply=%region_0.1 | reduce | flops 98304 | bytes 655364 | tf_op jit(solution)/shard_map/reduce_sum | solution.py:132
  37.4 1.9 %collective-permute-start.3 = (f32[4,32,256]{2,1,0:T(8,128)S(1)}, f32[4,32,256]{2,1,0:T(8,128)S(1)}, u32[]{:S(2)}, u32[]{:S(2)}) collective-permute-start(f32[4,32,256]{2,1,0:T(8,128)S(1)} %reduce_sum.9.refs_1_), channel_id=1, source_target_pairs={{0,8},{8,16},{16,24},{24,32},{32,40},{40,48},{48,56},{56,64},{64,7... | collective-permute-start | bytes 393224 | tf_op jit(solution)/shard_map/ppermute | solution.py:101
  39.4 3.9 %collective-permute-start.4 = (f32[4,32,256]{2,1,0:T(8,128)S(1)}, f32[4,32,256]{2,1,0:T(8,128)S(1)}, u32[]{:S(2)}, u32[]{:S(2)}) collective-permute-start(f32[4,32,256]{2,1,0:T(8,128)S(1)} %reduce_sum.9.refs_1_), channel_id=1, source_target_pairs={{8,0},{16,8},{24,16},{32,24},{40,32},{48,40},{56,48},{64,56},{72,6... | collective-permute-start | bytes 393224 | tf_op jit(solution)/shard_map/ppermute | solution.py:102
  43.3 0.0 collective-permute-done.5.refs_4_
  43.3 1.0 %collective-permute-done.3.refs_0_ = f32[4,32,256]{2,1,0:T(8,128)S(1)} collective-permute-done((f32[4,32,256]{2,1,0:T(8,128)S(1)}, f32[4,32,256]{2,1,0:T(8,128)S(1)}, u32[]{:S(2)}, u32[]{:S(2)}) %collective-permute-start.3) | collective-permute-done | bytes 131104 | tf_op jit(solution)/shard_map/ppermute | solution.py:101
  44.3 5.2 %collective-permute-done.4.refs_2_ = f32[4,32,256]{2,1,0:T(8,128)S(1)} collective-permute-done((f32[4,32,256]{2,1,0:T(8,128)S(1)}, f32[4,32,256]{2,1,0:T(8,128)S(1)}, u32[]{:S(2)}, u32[]{:S(2)}) %collective-permute-start.4) | collective-permute-done | bytes 131104 | tf_op jit(solution)/shard_map/ppermute | solution.py:102
  49.5 2.0 %shard_map.74 = f32[4,4,32,256]{3,2,1,0:T(8,128)S(1)} custom-call(f32[4,32,256]{2,1,0:T(8,128)S(1)} %collective-permute-done.3.refs_0_, f32[4,32,256]{2,1,0:T(8,128)S(1)} %reduce_sum.9.refs_1_, f32[4,32,256]{2,1,0:T(8,128)S(1)} %collective-permute-done.4.refs_2_, f32[1024,256]{1,0:T(8,128)S(1)} %bitcast.12, f32[1024,256]{1,0:T(8,128)} %collective-permute-done.5.refs_4_, ...), custom_call_target="tpu_custom_call" | custom-call | flops 268435456 | bytes 4194304 | tf_op jit(solution)/shard_map/pallas_call | solution.py:127
  51.5 10.5 %all_to_all.16.parts = f32[4,4,32,256]{3,2,1,0:T(8,128)S(1)} all-to-all(f32[4,4,32,256]{3,2,1,0:T(8,128)S(1)} %shard_map.74), channel_id=1, replica_groups=mesh['rows'=128,'x'=4,'core'=2] {'x'}, dimensions={0} | all-to-all | bytes 1048576 | tf_op jit(solution)/shard_map/all_to_all | solution.py:130
  62.0 0.7 shard_map.75
  62.7 1.9 %collective-permute-start.6 = (f32[4,32,256]{2,1,0:T(8,128)S(1)}, f32[4,32,256]{2,1,0:T(8,128)S(1)}, u32[]{:S(2)}, u32[]{:S(2)}) collective-permute-start(f32[4,32,256]{2,1,0:T(8,128)S(1)} %get-tuple-element.9), channel_id=1, source_target_pairs={{0,8},{8,16},{16,24},{24,32},{32,40},{40,48},{48,56},{56,64},{64,7... | collective-permute-start | bytes 393224 | tf_op jit(solution)/shard_map/ppermute | solution.py:101
  64.7 3.9 %collective-permute-start.7 = (f32[4,32,256]{2,1,0:T(8,128)S(1)}, f32[4,32,256]{2,1,0:T(8,128)S(1)}, u32[]{:S(2)}, u32[]{:S(2)}) collective-permute-start(f32[4,32,256]{2,1,0:T(8,128)S(1)} %get-tuple-element.10), channel_id=1, source_target_pairs={{8,0},{16,8},{24,16},{32,24},{40,32},{48,40},{56,48},{64,56},{72,6... | collective-permute-start | bytes 393224 | tf_op jit(solution)/shard_map/ppermute | solution.py:102
  68.6 1.0 %collective-permute-done.6.below = f32[4,32,256]{2,1,0:T(8,128)S(1)} collective-permute-done((f32[4,32,256]{2,1,0:T(8,128)S(1)}, f32[4,32,256]{2,1,0:T(8,128)S(1)}, u32[]{:S(2)}, u32[]{:S(2)}) %collective-permute-start.6) | collective-permute-done | bytes 131104 | tf_op jit(solution)/shard_map/ppermute | solution.py:101
  69.6 5.2 %collective-permute-done.7.above = f32[4,32,256]{2,1,0:T(8,128)S(1)} collective-permute-done((f32[4,32,256]{2,1,0:T(8,128)S(1)}, f32[4,32,256]{2,1,0:T(8,128)S(1)}, u32[]{:S(2)}, u32[]{:S(2)}) %collective-permute-start.7) | collective-permute-done | bytes 131104 | tf_op jit(solution)/shard_map/ppermute | solution.py:102
  74.8 0.2 shard_map.76
  75.0 8.5 %all_to_all.17.parts = f32[8,32,128]{2,1,0:T(8,128)S(1)} all-to-all(f32[8,32,128]{2,1,0:T(8,128)S(1)} %shard_map.76), channel_id=1, replica_groups=mesh['rows'=128,'x'=4,'core'=2] {'x','core'}, dimensions={0} | all-to-all | bytes 262144 | tf_op jit(solution)/shard_map/all_to_all | solution.py:141
  83.5 0.7 shard_map.77
  (1 shorter events, 0.0 us)
Async XLA Ops:
  0.0 7.7 %copy-start = (f32[4,256,64]{1,2,0:T(8,128)S(1)}, f32[4,256,64]{1,2,0:T(8,128)}, u32[]{:S(2)}) copy-start(f32[4,256,64]{1,2,0:T(8,128)} %param.13) | copy-start | bytes 786436
  0.9 4.4 %copy-start.2 = (f32[4,1,256,256]{3,2,1,0:T(8,128)S(1)}, f32[4,1,256,256]{3,2,1,0:T(8,128)}, u32[]{:S(2)}) copy-start(f32[4,1,256,256]{3,2,1,0:T(8,128)} %param.10) | copy-start | bytes 3145732
  0.9 21.9 %copy-start.1 = (f32[4,1,256,256]{3,2,1,0:T(8,128)S(1)}, f32[4,1,256,256]{3,2,1,0:T(8,128)}, u32[]{:S(2)}) copy-start(f32[4,1,256,256]{3,2,1,0:T(8,128)} %param.7) | copy-start | bytes 3145732
  3.4 19.4 %collective-permute-start.2 = (f32[1032,256]{1,0:T(8,128)}, f32[1032,256]{1,0:T(8,128)S(1)}, u32[]{:S(2)}, u32[]{:S(2)}) collective-permute-start(f32[1032,256]{1,0:T(8,128)} %pad_maximum_fusion), channel_id=1, source_target_pairs={{0,1},{1,0},{2,3},{3,2},{4,5},{5,4},{6,7},{7,6},{8,9},{9,8},{10,11... | collective-permute-start | bytes 3170312 | tf_op jit(solution)/shard_map/ppermute | solution.py:122
  5.3 38.0 %collective-permute-start.5 = (f32[1024,256]{1,0:T(8,128)S(1)}, f32[1024,256]{1,0:T(8,128)}, u32[]{:S(2)}, u32[]{:S(2)}) collective-permute-start(f32[1024,256]{1,0:T(8,128)S(1)} %bitcast.11), channel_id=1, source_target_pairs={{0,1},{1,0},{2,3},{3,2},{4,5},{5,4},{6,7},{7,6},{8,9},{9,8},{10,11... | collective-permute-start | bytes 3145736 | tf_op jit(solution)/shard_map/ppermute | solution.py:123
  7.7 7.6 %collective-permute-start = (f32[4,32,256]{2,1,0:T(8,128)S(1)}, f32[4,32,256]{2,1,0:T(8,128)S(1)}, u32[]{:S(2)}, u32[]{:S(2)}) collective-permute-start(f32[4,32,256]{2,1,0:T(8,128)S(1)} %dynamic-slice_bitcast_fusion.refs_1_), channel_id=1, source_target_pairs={{0,8},{8,16},{16,24},{24,32},{32,40},{40,48},{48,56},{56,64},{64,7... | collective-permute-start | bytes 393224 | tf_op jit(solution)/shard_map/ppermute | solution.py:101
  12.5 10.3 %collective-permute-start.1 = (f32[4,32,256]{2,1,0:T(8,128)S(1)}, f32[4,32,256]{2,1,0:T(8,128)S(1)}, u32[]{:S(2)}, u32[]{:S(2)}) collective-permute-start(f32[4,32,256]{2,1,0:T(8,128)S(1)} %dynamic-slice_bitcast_fusion.refs_1_), channel_id=1, source_target_pairs={{8,0},{16,8},{24,16},{32,24},{40,32},{48,40},{56,48},{64,56},{72,6... | collective-permute-start | bytes 393224 | tf_op jit(solution)/shard_map/ppermute | solution.py:102
  37.4 6.9 %collective-permute-start.3 = (f32[4,32,256]{2,1,0:T(8,128)S(1)}, f32[4,32,256]{2,1,0:T(8,128)S(1)}, u32[]{:S(2)}, u32[]{:S(2)}) collective-permute-start(f32[4,32,256]{2,1,0:T(8,128)S(1)} %reduce_sum.9.refs_1_), channel_id=1, source_target_pairs={{0,8},{8,16},{16,24},{24,32},{32,40},{40,48},{48,56},{56,64},{64,7... | collective-permute-start | bytes 393224 | tf_op jit(solution)/shard_map/ppermute | solution.py:101
  39.4 10.2 %collective-permute-start.4 = (f32[4,32,256]{2,1,0:T(8,128)S(1)}, f32[4,32,256]{2,1,0:T(8,128)S(1)}, u32[]{:S(2)}, u32[]{:S(2)}) collective-permute-start(f32[4,32,256]{2,1,0:T(8,128)S(1)} %reduce_sum.9.refs_1_), channel_id=1, source_target_pairs={{8,0},{16,8},{24,16},{32,24},{40,32},{48,40},{56,48},{64,56},{72,6... | collective-permute-start | bytes 393224 | tf_op jit(solution)/shard_map/ppermute | solution.py:102
  62.7 6.9 %collective-permute-start.6 = (f32[4,32,256]{2,1,0:T(8,128)S(1)}, f32[4,32,256]{2,1,0:T(8,128)S(1)}, u32[]{:S(2)}, u32[]{:S(2)}) collective-permute-start(f32[4,32,256]{2,1,0:T(8,128)S(1)} %get-tuple-element.9), channel_id=1, source_target_pairs={{0,8},{8,16},{16,24},{24,32},{32,40},{40,48},{48,56},{56,64},{64,7... | collective-permute-start | bytes 393224 | tf_op jit(solution)/shard_map/ppermute | solution.py:101
  64.7 10.2 %collective-permute-start.7 = (f32[4,32,256]{2,1,0:T(8,128)S(1)}, f32[4,32,256]{2,1,0:T(8,128)S(1)}, u32[]{:S(2)}, u32[]{:S(2)}) collective-permute-start(f32[4,32,256]{2,1,0:T(8,128)S(1)} %get-tuple-element.10), channel_id=1, source_target_pairs={{8,0},{16,8},{24,16},{32,24},{40,32},{48,40},{56,48},{64,56},{72,6... | collective-permute-start | bytes 393224 | tf_op jit(solution)/shard_map/ppermute | solution.py:102

commit v2 on v1

--- a/solution.py
+++ b/solution.py
@@ -59,6 +59,32 @@
                 ref[j] = ref[j] + jnp.where(where == w, term, 0.0)
 
 
+def fold_kernel(parts, out):
+    out[...] = (parts[0] + parts[1]) + (parts[2] + parts[3])
+
+
+def stage_kernel(*refs):
+    *small, z, out = refs[:6]
+    *local, sems = refs[6:]
+    copies = [pltpu.make_async_copy(a, b, sems.at[n]) for n, (a, b) in enumerate(zip(small, local))]
+    big = pltpu.make_async_copy(z, out.at[pl.ds(0, 1024)], sems.at[4])
+    for copy in copies + [big]:
+        copy.start()
+    for copy in copies:
+        copy.wait()
+    z_cols, z_count, h_cols, h_count = local
+    row = lax.axis_index("rows")
+    slot = lax.axis_index("x") * 2 + lax.axis_index("core")
+    turn = (row % 2) * 2 * HB
+    for line, (cols, count) in enumerate(((z_cols, z_count), (h_cols, h_count))):
+        for i in range(HB):
+            place = cols[i] - (row * HB - HB)
+            place = jnp.where(place < HB, place + turn, jnp.where(place < 2 * HB, place, place - turn))
+            place = jnp.where(slot < count[i], place, -1).astype(jnp.float32)
+            out[pl.ds(1024 + line * HB + i, 1), :] = jnp.full((1, 256), place, jnp.float32)
+    big.wait()
+
+
 def pack_kernel(own, below, above, out):
     for t in range(2):
         for j in range(HB):
@@ -96,48 +122,53 @@
     return jax.ShapeDtypeStruct(shape, jnp.float32)
 
 
-def neighbours(up, down):
+def neighbours(first, second):
     count = lax.axis_size("rows")
-    below = lax.ppermute(up, "rows", [(i, i + 1) for i in range(count - 1)])
-    above = lax.ppermute(down, "rows", [(i + 1, i) for i in range(count - 1)])
-    return below, above
+    results = []
+    for field, offset in ((first, 1), (second, 0)):
+        pairs = [(i, i + 1) for i in range(offset, count - 1, 2)]
+        results.append(lax.ppermute(field, "rows", pairs + [(b, a) for a, b in pairs]))
+    return results
 
 
 def steps(z_blocks, z_cols, z_count, h_blocks, h_cols, h_count, panel):
     q = lax.axis_index("core")
-    slot = lax.axis_index("x") * 2 + q
-    start = lax.axis_index("rows") * HB - HB
     z = z_blocks.reshape(1024, 256)
     h = h_blocks.reshape(1024, 256)
-
-    def index_rows(cols, count):
-        return jnp.where(slot < count, cols[:, 0] - start, -1)
-
-    index = jnp.concatenate([index_rows(z_cols, z_count), index_rows(h_cols, h_count)])
-    index = jnp.broadcast_to(index.astype(jnp.float32)[:, None], (8, 256))
+    hbm = pl.BlockSpec(memory_space=pltpu.HBM)
+    operands = (z_cols.reshape(HB), z_count, h_cols.reshape(HB), h_count, z)
+    mine = pl.pallas_call(
+        stage_kernel,
+        out_shape=f32(1032, 256),
+        in_specs=[hbm] * 5,
+        out_specs=VMEM,
+        scratch_shapes=[pltpu.SMEM((HB,), jnp.int32)] * 4 + [pltpu.SemaphoreType.DMA((5,))],
+        compiler_params=pltpu.CompilerParams(vmem_limit_bytes=4 << 20),
+        name="stage",
+    )(*(pltpu.with_memory_space_constraint(a, pltpu.HBM) for a in operands))
+    mine, panel = lax.optimization_barrier((mine, panel))
 
     swap = [(0, 1), (1, 0)]
     x = lax.dynamic_slice_in_dim(jnp.swapaxes(panel, 1, 2), q * 32, 32, axis=1)
-    x_low, x_high = neighbours(x, x)
-    theirs = lax.ppermute(jnp.concatenate([z, index], axis=0), "core", swap)
+    x_first, x_second = neighbours(x, x)
+    theirs = lax.ppermute(mine, "core", swap)
     h_theirs = lax.ppermute(h, "core", swap)
 
-    def forward(row, low, own, high, mine, other):
-        body = lambda *refs: forward_kernel(row, *refs)
-        return call(body, f32(4, HB, 32, 256), 7, 1 << 28, 1 << 22)(low, own, high, mine, other, index, theirs)
-
-    def exchange(parts):
+    def forward(line, first, own, second, blocks, other):
+        body = lambda *refs: forward_kernel(line, *refs)
+        parts = call(body, f32(4, HB, 32, 256), 7, 1 << 28, 1 << 22)(first, own, second, blocks, other, mine, theirs)
         return lax.all_to_all(parts, "x", 0, 0, tiled=True)
 
-    mid = exchange(forward(0, x_low, x, x_high, z, theirs)).sum(axis=0)
-    mid_low, mid_high = neighbours(mid, mid)
-    side = exchange(forward(4, mid_low, mid, mid_high, h, h_theirs))
+    mid = forward(0, x_first, x, x_second, mine, theirs)
+    mid = call(fold_kernel, f32(HB, 32, 256), 1, 1 << 18, 1 << 19)(mid)
+    mid_first, mid_second = neighbours(mid, mid)
+    side = forward(4, mid_first, mid, mid_second, h, h_theirs)
     shape = f32(HB, 32, 256)
-    low, own, high = call(backward_kernel, (shape, shape, shape), 5, 1 << 28, 1 << 22)(
-        side, z, theirs, index, theirs
+    first, own, second = call(backward_kernel, (shape, shape, shape), 5, 1 << 28, 1 << 22)(
+        side, mine, theirs, mine, theirs
     )
-    from_below, from_above = neighbours(high, low)
-    packed = call(pack_kernel, f32(8, 32, 128), 3, 1 << 20, 1 << 20)(own, from_below, from_above)
+    first, second = neighbours(first, second)
+    packed = call(pack_kernel, f32(8, 32, 128), 3, 1 << 20, 1 << 20)(own, first, second)
     arrived = lax.all_to_all(packed, ("x", "core"), 0, 0, tiled=True)
     return call(final_kernel, f32(HB, 32, 64), 1, 1 << 20, 1 << 18)(arrived)
 

time: 84.7 us -> 80.5 us (0.950)
  the two profiles are of different devices: /device:TPU:504 before, /device:TPU:1 now
where the time goes in v2:
time: 80.5 us; the launch traced here: 80.1 us
  blocking collectives  33 us (41%)
  starting transfers between devices  31.9 us (40%)
  waiting for transfers between devices  9.18 us (11%)
  Pallas kernels  5.81 us (7%)
    all_to_all x2, blocking collectives, forward(): return lax.all_to_all(parts, 'x', 0, 0, tiled=True)  19.7 us
    ppermute x1, starting transfers between devices, steps(): theirs = lax.ppermute(mine, 'core', swap)  16 us
    ppermute x6, starting transfers between devices, neighbours(): lax.ppermute(field, 'rows', pairs + [(b, a) for a, b in pairs])  14 us
    all_to_all x1, blocking collectives, steps(): arrived = lax.all_to_all(packed, ('x', 'core'), 0, 0, tiled=True)  13.3 us
    ppermute x6, waiting for transfers between devices, neighbours(): lax.ppermute(field, 'rows', pairs + [(b, a) for a, b in pairs])  9.17 us
    pallas_call x2, Pallas kernels, forward(): call(body, f32(4, HB, 32, 256), 7, 1 << 28, 1 << 22)  2.77 us
    ppermute x1, starting transfers between devices, steps(): h_theirs = lax.ppermute(h, 'core', swap)  1.92 us
  transfers between devices with their start and end apart: 8, of which 3 were waited for; matrix products, arithmetic and copies ran while one was open for 0% of the time, Pallas kernels for 1%

profile of v2, /device:TPU:1, one launch (start us, length us, event | category | flops | bytes accessed | tf_op | source)
XLA Modules:
  0.0 80.1 jit_solution(16779147627314524785)
XLA Ops:
  0.0 0.0 copy-start
  0.0 0.0 copy-start.1
  0.0 1.4 %stage.1.refs_3_.refs_5_.mine.index_mine = f32[1032,256]{1,0:T(8,128)S(1)} custom-call(s32[4]{0:T(128)} %bitcast.9, s32[4]{0:T(128)} %refs_1_.1, s32[4]{0:T(128)} %bitcast.10, s32[4]{0:T(128)} %refs_3_.1, f32[1024,256]{1,0:T(8,128)} %bitcast.8), custom_call_target="tpu_custom_call" | custom-call | tf_op jit(solution)/shard_map/stage/pallas_call | solution.py:140
  1.4 16.0 %collective-permute-start.2 = (f32[1032,256]{1,0:T(8,128)S(1)}, f32[1032,256]{1,0:T(8,128)S(1)}, u32[]{:S(2)}, u32[]{:S(2)}) collective-permute-start(f32[1032,256]{1,0:T(8,128)S(1)} %stage.1.refs_3_.refs_5_.mine.index_mine), channel_id=1, source_target_pairs={{0,1},{1,0},{2,3},{3,2},{4,5},{5,4},{6,7},{7,6},{8,9},{9,8},{10,11... | collective-permute-start | bytes 3170312 | tf_op jit(solution)/shard_map/ppermute | solution.py:154
  17.4 0.0 copy-done.1
  17.4 1.9 %collective-permute-start.5 = (f32[1024,256]{1,0:T(8,128)S(1)}, f32[1024,256]{1,0:T(8,128)}, u32[]{:S(2)}, u32[]{:S(2)}) collective-permute-start(f32[1024,256]{1,0:T(8,128)S(1)} %bitcast.6), channel_id=1, source_target_pairs={{0,1},{1,0},{2,3},{3,2},{4,5},{5,4},{6,7},{7,6},{8,9},{9,8},{10,11... | collective-permute-start | bytes 3145736 | tf_op jit(solution)/shard_map/ppermute | solution.py:155
  19.4 0.0 copy-done
  19.4 0.7 collective-permute-start
  20.1 1.9 %collective-permute-start.1 = (f32[4,32,256]{2,1,0:T(8,128)S(1)}, f32[4,32,256]{2,1,0:T(8,128)S(1)}, u32[]{:S(2)}, u32[]{:S(2)}) collective-permute-start(f32[4,32,256]{2,1,0:T(8,128)S(1)} %dynamic-slice_bitcast_fusion.refs_1_), channel_id=1, source_target_pairs={{0,8},{16,24},{32,40},{48,56},{64,72},{80,88},{96,104},{112,120},{... | collective-permute-start | bytes 393224 | tf_op jit(solution)/shard_map/ppermute | solution.py:130
  22.0 0.0 collective-permute-done.refs_0_
  22.0 4.5 %collective-permute-done.1.refs_2_ = f32[4,32,256]{2,1,0:T(8,128)S(1)} collective-permute-done((f32[4,32,256]{2,1,0:T(8,128)S(1)}, f32[4,32,256]{2,1,0:T(8,128)S(1)}, u32[]{:S(2)}, u32[]{:S(2)}) %collective-permute-start.1) | collective-permute-done | bytes 131104 | tf_op jit(solution)/shard_map/ppermute | solution.py:130
  26.5 0.0 collective-permute-done.2.refs_4_.refs_6_.theirs.index_theirs
  26.5 0.8 shard_map.73
  27.3 10.3 %all_to_all.15.parts = f32[4,4,32,256]{3,2,1,0:T(8,128)S(1)} all-to-all(f32[4,4,32,256]{3,2,1,0:T(8,128)S(1)} %shard_map.73), channel_id=1, replica_groups=mesh['rows'=128,'x'=4,'core'=2] {'x'}, dimensions={0} | all-to-all | bytes 1048576 | tf_op jit(solution)/shard_map/all_to_all | solution.py:160
  37.7 0.7 collective-permute-start.3
  38.4 4.0 %collective-permute-start.4 = (f32[4,32,256]{2,1,0:T(8,128)S(1)}, f32[4,32,256]{2,1,0:T(8,128)S(1)}, u32[]{:S(2)}, u32[]{:S(2)}) collective-permute-start(f32[4,32,256]{2,1,0:T(8,128)S(1)} %shard_map.74.refs_1_), channel_id=1, source_target_pairs={{0,8},{16,24},{32,40},{48,56},{64,72},{80,88},{96,104},{112,120},{... | collective-permute-start | bytes 393224 | tf_op jit(solution)/shard_map/ppermute | solution.py:130
  42.4 0.0 collective-permute-done.5.refs_4_
  42.4 0.0 collective-permute-done.3.refs_0_
  42.4 2.3 %collective-permute-done.4.refs_2_ = f32[4,32,256]{2,1,0:T(8,128)S(1)} collective-permute-done((f32[4,32,256]{2,1,0:T(8,128)S(1)}, f32[4,32,256]{2,1,0:T(8,128)S(1)}, u32[]{:S(2)}, u32[]{:S(2)}) %collective-permute-start.4) | collective-permute-done | bytes 131104 | tf_op jit(solution)/shard_map/ppermute | solution.py:130
  44.7 2.0 %shard_map.75 = f32[4,4,32,256]{3,2,1,0:T(8,128)S(1)} custom-call(f32[4,32,256]{2,1,0:T(8,128)S(1)} %collective-permute-done.3.refs_0_, f32[4,32,256]{2,1,0:T(8,128)S(1)} %shard_map.74.refs_1_, f32[4,32,256]{2,1,0:T(8,128)S(1)} %collective-permute-done.4.refs_2_, f32[1024,256]{1,0:T(8,128)S(1)} %bitcast.7, f32[1024,256]{1,0:T(8,128)} %collective-permute-done.5.refs_4_, ...), custom_call_target="tpu_custom_call" | custom-call | flops 268435456 | bytes 4194304 | tf_op jit(solution)/shard_map/pallas_call | solution.py:159
  46.7 9.3 %all_to_all.16.parts = f32[4,4,32,256]{3,2,1,0:T(8,128)S(1)} all-to-all(f32[4,4,32,256]{3,2,1,0:T(8,128)S(1)} %shard_map.75), channel_id=1, replica_groups=mesh['rows'=128,'x'=4,'core'=2] {'x'}, dimensions={0} | all-to-all | bytes 1048576 | tf_op jit(solution)/shard_map/all_to_all | solution.py:160
  56.0 0.7 shard_map.76
  56.8 0.7 collective-permute-start.6
  57.5 6.1 %collective-permute-start.7 = (f32[4,32,256]{2,1,0:T(8,128)S(1)}, f32[4,32,256]{2,1,0:T(8,128)S(1)}, u32[]{:S(2)}, u32[]{:S(2)}) collective-permute-start(f32[4,32,256]{2,1,0:T(8,128)S(1)} %get-tuple-element.14), channel_id=1, source_target_pairs={{0,8},{16,24},{32,40},{48,56},{64,72},{80,88},{96,104},{112,120},{... | collective-permute-start | bytes 393224 | tf_op jit(solution)/shard_map/ppermute | solution.py:130
  63.5 0.0 collective-permute-done.6.below
  63.5 2.3 %collective-permute-done.7.above = f32[4,32,256]{2,1,0:T(8,128)S(1)} collective-permute-done((f32[4,32,256]{2,1,0:T(8,128)S(1)}, f32[4,32,256]{2,1,0:T(8,128)S(1)}, u32[]{:S(2)}, u32[]{:S(2)}) %collective-permute-start.7) | collective-permute-done | bytes 131104 | tf_op jit(solution)/shard_map/ppermute | solution.py:130
  65.9 0.2 shard_map.77
  66.1 13.3 %all_to_all.17.parts = f32[8,32,128]{2,1,0:T(8,128)S(1)} all-to-all(f32[8,32,128]{2,1,0:T(8,128)S(1)} %shard_map.77), channel_id=1, replica_groups=mesh['rows'=128,'x'=4,'core'=2] {'x','core'}, dimensions={0} | all-to-all | bytes 262144 | tf_op jit(solution)/shard_map/all_to_all | solution.py:172
  79.3 0.7 shard_map.78
  (2 shorter events, 0.0 us)
Async XLA Ops:
  0.0 19.4 %copy-start = (f32[4,256,64]{1,2,0:T(8,128)S(1)}, f32[4,256,64]{1,2,0:T(8,128)}, u32[]{:S(2)}) copy-start(f32[4,256,64]{1,2,0:T(8,128)} %param.13) | copy-start | bytes 786436
  0.0 17.4 %copy-start.1 = (f32[4,1,256,256]{3,2,1,0:T(8,128)S(1)}, f32[4,1,256,256]{3,2,1,0:T(8,128)}, u32[]{:S(2)}) copy-start(f32[4,1,256,256]{3,2,1,0:T(8,128)} %param.10) | copy-start | bytes 3145732
  1.4 25.1 %collective-permute-start.2 = (f32[1032,256]{1,0:T(8,128)S(1)}, f32[1032,256]{1,0:T(8,128)S(1)}, u32[]{:S(2)}, u32[]{:S(2)}) collective-permute-start(f32[1032,256]{1,0:T(8,128)S(1)} %stage.1.refs_3_.refs_5_.mine.index_mine), channel_id=1, source_target_pairs={{0,1},{1,0},{2,3},{3,2},{4,5},{5,4},{6,7},{7,6},{8,9},{9,8},{10,11... | collective-permute-start | bytes 3170312 | tf_op jit(solution)/shard_map/ppermute | solution.py:154
  17.4 25.0 %collective-permute-start.5 = (f32[1024,256]{1,0:T(8,128)S(1)}, f32[1024,256]{1,0:T(8,128)}, u32[]{:S(2)}, u32[]{:S(2)}) collective-permute-start(f32[1024,256]{1,0:T(8,128)S(1)} %bitcast.6), channel_id=1, source_target_pairs={{0,1},{1,0},{2,3},{3,2},{4,5},{5,4},{6,7},{7,6},{8,9},{9,8},{10,11... | collective-permute-start | bytes 3145736 | tf_op jit(solution)/shard_map/ppermute | solution.py:155
  19.4 2.6 %collective-permute-start = (f32[4,32,256]{2,1,0:T(8,128)S(1)}, f32[4,32,256]{2,1,0:T(8,128)S(1)}, u32[]{:S(2)}, u32[]{:S(2)}) collective-permute-start(f32[4,32,256]{2,1,0:T(8,128)S(1)} %dynamic-slice_bitcast_fusion.refs_1_), channel_id=1, source_target_pairs={{8,16},{24,32},{40,48},{56,64},{72,80},{88,96},{104,112},{120,128}... | collective-permute-start | bytes 393224 | tf_op jit(solution)/shard_map/ppermute | solution.py:130
  20.1 6.5 %collective-permute-start.1 = (f32[4,32,256]{2,1,0:T(8,128)S(1)}, f32[4,32,256]{2,1,0:T(8,128)S(1)}, u32[]{:S(2)}, u32[]{:S(2)}) collective-permute-start(f32[4,32,256]{2,1,0:T(8,128)S(1)} %dynamic-slice_bitcast_fusion.refs_1_), channel_id=1, source_target_pairs={{0,8},{16,24},{32,40},{48,56},{64,72},{80,88},{96,104},{112,120},{... | collective-permute-start | bytes 393224 | tf_op jit(solution)/shard_map/ppermute | solution.py:130
  37.7 4.7 %collective-permute-start.3 = (f32[4,32,256]{2,1,0:T(8,128)S(1)}, f32[4,32,256]{2,1,0:T(8,128)S(1)}, u32[]{:S(2)}, u32[]{:S(2)}) collective-permute-start(f32[4,32,256]{2,1,0:T(8,128)S(1)} %shard_map.74.refs_1_), channel_id=1, source_target_pairs={{8,16},{24,32},{40,48},{56,64},{72,80},{88,96},{104,112},{120,128}... | collective-permute-start | bytes 393224 | tf_op jit(solution)/shard_map/ppermute | solution.py:130
  38.4 6.4 %collective-permute-start.4 = (f32[4,32,256]{2,1,0:T(8,128)S(1)}, f32[4,32,256]{2,1,0:T(8,128)S(1)}, u32[]{:S(2)}, u32[]{:S(2)}) collective-permute-start(f32[4,32,256]{2,1,0:T(8,128)S(1)} %shard_map.74.refs_1_), channel_id=1, source_target_pairs={{0,8},{16,24},{32,40},{48,56},{64,72},{80,88},{96,104},{112,120},{... | collective-permute-start | bytes 393224 | tf_op jit(solution)/shard_map/ppermute | solution.py:130
  56.8 6.7 %collective-permute-start.6 = (f32[4,32,256]{2,1,0:T(8,128)S(1)}, f32[4,32,256]{2,1,0:T(8,128)S(1)}, u32[]{:S(2)}, u32[]{:S(2)}) collective-permute-start(f32[4,32,256]{2,1,0:T(8,128)S(1)} %get-tuple-element.13), channel_id=1, source_target_pairs={{8,16},{24,32},{40,48},{56,64},{72,80},{88,96},{104,112},{120,128}... | collective-permute-start | bytes 393224 | tf_op jit(solution)/shard_map/ppermute | solution.py:130
  57.5 8.4 %collective-permute-start.7 = (f32[4,32,256]{2,1,0:T(8,128)S(1)}, f32[4,32,256]{2,1,0:T(8,128)S(1)}, u32[]{:S(2)}, u32[]{:S(2)}) collective-permute-start(f32[4,32,256]{2,1,0:T(8,128)S(1)} %get-tuple-element.14), channel_id=1, source_target_pairs={{0,8},{16,24},{32,40},{48,56},{64,72},{80,88},{96,104},{112,120},{... | collective-permute-start | bytes 393224 | tf_op jit(solution)/shard_map/ppermute | solution.py:130

commit v3 on v2

--- a/solution.py
+++ b/solution.py
@@ -35,11 +35,12 @@
 def forward_kernel(row, low, own, high, mine, theirs, index_mine, index_theirs, out):
     n = own.shape[1]
     fields = [ref[j] for ref in (low, own, high) for j in range(HB)]
+    turned = fields[2 * HB :] + fields[HB : 2 * HB] + fields[:HB]
     for i in range(HB):
         total = None
-        for blocks, index in ((mine, index_mine), (theirs, index_theirs)):
+        for blocks, index, window in ((mine, index_mine, fields), (theirs, index_theirs, turned)):
             where = jnp.broadcast_to(index[pl.ds(index.shape[0] - 8 + row + i, 1), :], (n, 256))
-            part = product(pick(fields, where), blocks[pl.ds(i * 256, 256), :], ((1,), (1,)))
+            part = product(pick(window, where), blocks[pl.ds(i * 256, 256), :], ((1,), (1,)))
             total = part if total is None else total + part
         for x in range(out.shape[0]):
             out[x, i] = total
@@ -48,14 +49,15 @@
 def backward_kernel(parts, mine, theirs, index_mine, index_theirs, low, own, high):
     n = own.shape[1]
     outs = [(ref, j) for ref in (low, own, high) for j in range(HB)]
+    turned = outs[2 * HB :] + outs[HB : 2 * HB] + outs[:HB]
     for ref, j in outs:
         ref[j] = jnp.zeros((n, 256), jnp.float32)
     for i in range(HB):
         side = (parts[0, i] + parts[1, i]) + (parts[2, i] + parts[3, i])
-        for blocks, index in ((mine, index_mine), (theirs, index_theirs)):
+        for blocks, index, window in ((mine, index_mine, outs), (theirs, index_theirs, turned)):
             where = jnp.broadcast_to(index[pl.ds(index.shape[0] - 8 + i, 1), :], (n, 256))
             term = product(side, blocks[pl.ds(i * 256, 256), :], ((1,), (0,)))
-            for w, (ref, j) in enumerate(outs):
+            for w, (ref, j) in enumerate(window):
                 ref[j] = ref[j] + jnp.where(where == w, term, 0.0)
 
 
@@ -75,7 +77,7 @@
     z_cols, z_count, h_cols, h_count = local
     row = lax.axis_index("rows")
     slot = lax.axis_index("x") * 2 + lax.axis_index("core")
-    turn = (row % 2) * 2 * HB
+    turn = ((row + lax.axis_index("core")) % 2) * 2 * HB
     for line, (cols, count) in enumerate(((z_cols, z_count), (h_cols, h_count))):
         for i in range(HB):
             place = cols[i] - (row * HB - HB)
@@ -125,9 +127,11 @@
 def neighbours(first, second):
     count = lax.axis_size("rows")
     results = []
-    for field, offset in ((first, 1), (second, 0)):
-        pairs = [(i, i + 1) for i in range(offset, count - 1, 2)]
-        results.append(lax.ppermute(field, "rows", pairs + [(b, a) for a, b in pairs]))
+    for field, step in ((first, 0), (second, 1)):
+        pairs = []
+        for core in range(2):
+            pairs += [(2 * i + core, 2 * i + 2 + core) for i in range((core + step + 1) % 2, count - 1, 2)]
+        results.append(lax.ppermute(field, ("rows", "core"), pairs + [(b, a) for a, b in pairs]))
     return results
 
 

time: 80.5 us -> 81 us (level)
  the two profiles are of different devices: /device:TPU:1 before, /device:TPU:768 now
where the time goes in v3:
time: 81 us; the launch traced here: 80.5 us
  blocking collectives  32.2 us (40%)
  starting transfers between devices  27.5 us (34%)
  waiting for transfers between devices  14.8 us (18%)
  Pallas kernels  5.81 us (7%)
    all_to_all x2, blocking collectives, forward(): return lax.all_to_all(parts, 'x', 0, 0, tiled=True)  23.7 us
    ppermute x6, starting transfers between devices, neighbours(): lax.ppermute(field, ('rows', 'core'), pairs + [(b, a) for a, b in pairs])  23.2 us
    ppermute x6, waiting for transfers between devices, neighbours(): lax.ppermute(field, ('rows', 'core'), pairs + [(b, a) for a, b in pairs])  14.8 us
    all_to_all x1, blocking collectives, steps(): arrived = lax.all_to_all(packed, ('x', 'core'), 0, 0, tiled=True)  8.49 us
    pallas_call x2, Pallas kernels, forward(): call(body, f32(4, HB, 32, 256), 7, 1 << 28, 1 << 22)  2.77 us
    ppermute x1, starting transfers between devices, steps(): h_theirs = lax.ppermute(h, 'core', swap)  2.41 us
    ppermute x1, starting transfers between devices, steps(): theirs = lax.ppermute(mine, 'core', swap)  1.92 us
  transfers between devices with their start and end apart: 8, of which 6 were waited for; matrix products, arithmetic and copies ran while one was open for 0% of the time, Pallas kernels for 1%

profile of v3, /device:TPU:768, one launch (start us, length us, event | category | flops | bytes accessed | tf_op | source)
XLA Modules:
  0.0 80.5 jit_solution(14064271987260142000)
XLA Ops:
  0.0 0.0 copy-start
  0.0 0.0 copy-start.1
  0.0 1.4 %stage.1.refs_3_.refs_5_.mine.index_mine = f32[1032,256]{1,0:T(8,128)S(1)} custom-call(s32[4]{0:T(128)} %bitcast.9, s32[4]{0:T(128)} %refs_1_.1, s32[4]{0:T(128)} %bitcast.10, s32[4]{0:T(128)} %refs_3_.1, f32[1024,256]{1,0:T(8,128)} %bitcast.8), custom_call_target="tpu_custom_call" | custom-call | tf_op jit(solution)/shard_map/stage/pallas_call | solution.py:144
  1.4 1.9 %collective-permute-start.2 = (f32[1032,256]{1,0:T(8,128)S(1)}, f32[1032,256]{1,0:T(8,128)S(1)}, u32[]{:S(2)}, u32[]{:S(2)}) collective-permute-start(f32[1032,256]{1,0:T(8,128)S(1)} %stage.1.refs_3_.refs_5_.mine.index_mine), channel_id=1, source_target_pairs={{0,1},{1,0},{2,3},{3,2},{4,5},{5,4},{6,7},{7,6},{8,9},{9,8},{10,11... | collective-permute-start | bytes 3170312 | tf_op jit(solution)/shard_map/ppermute | solution.py:158
  3.3 0.0 copy-done.1
  3.3 2.4 %collective-permute-start.5 = (f32[1024,256]{1,0:T(8,128)S(1)}, f32[1024,256]{1,0:T(8,128)}, u32[]{:S(2)}, u32[]{:S(2)}) collective-permute-start(f32[1024,256]{1,0:T(8,128)S(1)} %bitcast.6), channel_id=1, source_target_pairs={{0,1},{1,0},{2,3},{3,2},{4,5},{5,4},{6,7},{7,6},{8,9},{9,8},{10,11... | collective-permute-start | bytes 3145736 | tf_op jit(solution)/shard_map/ppermute | solution.py:159
  5.7 0.0 copy-done
  5.8 6.6 %collective-permute-start = (f32[4,32,256]{2,1,0:T(8,128)S(1)}, f32[4,32,256]{2,1,0:T(8,128)S(1)}, u32[]{:S(2)}, u32[]{:S(2)}) collective-permute-start(f32[4,32,256]{2,1,0:T(8,128)S(1)} %dynamic-slice_bitcast_fusion.refs_1_), channel_id=1, source_target_pairs={{8,16},{24,32},{40,48},{56,64},{72,80},{88,96},{104,112},{120,128}... | collective-permute-start | bytes 393224 | tf_op jit(solution)/shard_map/ppermute | solution.py:134
  12.4 1.9 %collective-permute-start.1 = (f32[4,32,256]{2,1,0:T(8,128)S(1)}, f32[4,32,256]{2,1,0:T(8,128)S(1)}, u32[]{:S(2)}, u32[]{:S(2)}) collective-permute-start(f32[4,32,256]{2,1,0:T(8,128)S(1)} %dynamic-slice_bitcast_fusion.refs_1_), channel_id=1, source_target_pairs={{0,8},{16,24},{32,40},{48,56},{64,72},{80,88},{96,104},{112,120},{... | collective-permute-start | bytes 393224 | tf_op jit(solution)/shard_map/ppermute | solution.py:134
  14.3 1.7 %collective-permute-done.refs_0_ = f32[4,32,256]{2,1,0:T(8,128)S(1)} collective-permute-done((f32[4,32,256]{2,1,0:T(8,128)S(1)}, f32[4,32,256]{2,1,0:T(8,128)S(1)}, u32[]{:S(2)}, u32[]{:S(2)}) %collective-permute-start) | collective-permute-done | bytes 131104 | tf_op jit(solution)/shard_map/ppermute | solution.py:134
  16.0 3.3 %collective-permute-done.1.refs_2_ = f32[4,32,256]{2,1,0:T(8,128)S(1)} collective-permute-done((f32[4,32,256]{2,1,0:T(8,128)S(1)}, f32[4,32,256]{2,1,0:T(8,128)S(1)}, u32[]{:S(2)}, u32[]{:S(2)}) %collective-permute-start.1) | collective-permute-done | bytes 131104 | tf_op jit(solution)/shard_map/ppermute | solution.py:134
  19.2 0.0 collective-permute-done.2.refs_4_.refs_6_.theirs.index_theirs
  19.2 0.8 shard_map.73
  20.0 12.5 %all_to_all.15.parts = f32[4,4,32,256]{3,2,1,0:T(8,128)S(1)} all-to-all(f32[4,4,32,256]{3,2,1,0:T(8,128)S(1)} %shard_map.73), channel_id=1, replica_groups=mesh['rows'=128,'x'=4,'core'=2] {'x'}, dimensions={0} | all-to-all | bytes 1048576 | tf_op jit(solution)/shard_map/all_to_all | solution.py:164
  32.6 5.2 %collective-permute-start.3 = (f32[4,32,256]{2,1,0:T(8,128)S(1)}, f32[4,32,256]{2,1,0:T(8,128)S(1)}, u32[]{:S(2)}, u32[]{:S(2)}) collective-permute-start(f32[4,32,256]{2,1,0:T(8,128)S(1)} %shard_map.74.refs_1_), channel_id=1, source_target_pairs={{8,16},{24,32},{40,48},{56,64},{72,80},{88,96},{104,112},{120,128}... | collective-permute-start | bytes 393224 | tf_op jit(solution)/shard_map/ppermute | solution.py:134
  37.8 1.9 %collective-permute-start.4 = (f32[4,32,256]{2,1,0:T(8,128)S(1)}, f32[4,32,256]{2,1,0:T(8,128)S(1)}, u32[]{:S(2)}, u32[]{:S(2)}) collective-permute-start(f32[4,32,256]{2,1,0:T(8,128)S(1)} %shard_map.74.refs_1_), channel_id=1, source_target_pairs={{0,8},{16,24},{32,40},{48,56},{64,72},{80,88},{96,104},{112,120},{... | collective-permute-start | bytes 393224 | tf_op jit(solution)/shard_map/ppermute | solution.py:134
  39.7 0.0 collective-permute-done.5.refs_4_
  39.7 4.1 %collective-permute-done.3.refs_0_ = f32[4,32,256]{2,1,0:T(8,128)S(1)} collective-permute-done((f32[4,32,256]{2,1,0:T(8,128)S(1)}, f32[4,32,256]{2,1,0:T(8,128)S(1)}, u32[]{:S(2)}, u32[]{:S(2)}) %collective-permute-start.3) | collective-permute-done | bytes 131104 | tf_op jit(solution)/shard_map/ppermute | solution.py:134
  43.8 0.9 %collective-permute-done.4.refs_2_ = f32[4,32,256]{2,1,0:T(8,128)S(1)} collective-permute-done((f32[4,32,256]{2,1,0:T(8,128)S(1)}, f32[4,32,256]{2,1,0:T(8,128)S(1)}, u32[]{:S(2)}, u32[]{:S(2)}) %collective-permute-start.4) | collective-permute-done | bytes 131104 | tf_op jit(solution)/shard_map/ppermute | solution.py:134
  44.6 2.0 %shard_map.75 = f32[4,4,32,256]{3,2,1,0:T(8,128)S(1)} custom-call(f32[4,32,256]{2,1,0:T(8,128)S(1)} %collective-permute-done.3.refs_0_, f32[4,32,256]{2,1,0:T(8,128)S(1)} %shard_map.74.refs_1_, f32[4,32,256]{2,1,0:T(8,128)S(1)} %collective-permute-done.4.refs_2_, f32[1024,256]{1,0:T(8,128)S(1)} %bitcast.7, f32[1024,256]{1,0:T(8,128)} %collective-permute-done.5.refs_4_, ...), custom_call_target="tpu_custom_call" | custom-call | flops 268435456 | bytes 4194304 | tf_op jit(solution)/shard_map/pallas_call | solution.py:163
  46.6 11.1 %all_to_all.16.parts = f32[4,4,32,256]{3,2,1,0:T(8,128)S(1)} all-to-all(f32[4,4,32,256]{3,2,1,0:T(8,128)S(1)} %shard_map.75), channel_id=1, replica_groups=mesh['rows'=128,'x'=4,'core'=2] {'x'}, dimensions={0} | all-to-all | bytes 1048576 | tf_op jit(solution)/shard_map/all_to_all | solution.py:164
  57.7 0.7 shard_map.76
  58.5 5.7 %collective-permute-start.6 = (f32[4,32,256]{2,1,0:T(8,128)S(1)}, f32[4,32,256]{2,1,0:T(8,128)S(1)}, u32[]{:S(2)}, u32[]{:S(2)}) collective-permute-start(f32[4,32,256]{2,1,0:T(8,128)S(1)} %get-tuple-element.13), channel_id=1, source_target_pairs={{8,16},{24,32},{40,48},{56,64},{72,80},{88,96},{104,112},{120,128}... | collective-permute-start | bytes 393224 | tf_op jit(solution)/shard_map/ppermute | solution.py:134
  64.2 1.9 %collective-permute-start.7 = (f32[4,32,256]{2,1,0:T(8,128)S(1)}, f32[4,32,256]{2,1,0:T(8,128)S(1)}, u32[]{:S(2)}, u32[]{:S(2)}) collective-permute-start(f32[4,32,256]{2,1,0:T(8,128)S(1)} %get-tuple-element.14), channel_id=1, source_target_pairs={{0,8},{16,24},{32,40},{48,56},{64,72},{80,88},{96,104},{112,120},{... | collective-permute-start | bytes 393224 | tf_op jit(solution)/shard_map/ppermute | solution.py:134
  66.2 3.0 %collective-permute-done.6.below = f32[4,32,256]{2,1,0:T(8,128)S(1)} collective-permute-done((f32[4,32,256]{2,1,0:T(8,128)S(1)}, f32[4,32,256]{2,1,0:T(8,128)S(1)}, u32[]{:S(2)}, u32[]{:S(2)}) %collective-permute-start.6) | collective-permute-done | bytes 131104 | tf_op jit(solution)/shard_map/ppermute | solution.py:134
  69.2 1.9 %collective-permute-done.7.above = f32[4,32,256]{2,1,0:T(8,128)S(1)} collective-permute-done((f32[4,32,256]{2,1,0:T(8,128)S(1)}, f32[4,32,256]{2,1,0:T(8,128)S(1)}, u32[]{:S(2)}, u32[]{:S(2)}) %collective-permute-start.7) | collective-permute-done | bytes 131104 | tf_op jit(solution)/shard_map/ppermute | solution.py:134
  71.1 0.2 shard_map.77
  71.3 8.5 %all_to_all.17.parts = f32[8,32,128]{2,1,0:T(8,128)S(1)} all-to-all(f32[8,32,128]{2,1,0:T(8,128)S(1)} %shard_map.77), channel_id=1, replica_groups=mesh['rows'=128,'x'=4,'core'=2] {'x','core'}, dimensions={0} | all-to-all | bytes 262144 | tf_op jit(solution)/shard_map/all_to_all | solution.py:176
  79.8 0.7 shard_map.78
  (2 shorter events, 0.0 us)
Async XLA Ops:
  0.0 5.7 %copy-start = (f32[4,256,64]{1,2,0:T(8,128)S(1)}, f32[4,256,64]{1,2,0:T(8,128)}, u32[]{:S(2)}) copy-start(f32[4,256,64]{1,2,0:T(8,128)} %param.13) | copy-start | bytes 786436
  0.0 3.3 %copy-start.1 = (f32[4,1,256,256]{3,2,1,0:T(8,128)S(1)}, f32[4,1,256,256]{3,2,1,0:T(8,128)}, u32[]{:S(2)}) copy-start(f32[4,1,256,256]{3,2,1,0:T(8,128)} %param.10) | copy-start | bytes 3145732
  1.4 17.8 %collective-permute-start.2 = (f32[1032,256]{1,0:T(8,128)S(1)}, f32[1032,256]{1,0:T(8,128)S(1)}, u32[]{:S(2)}, u32[]{:S(2)}) collective-permute-start(f32[1032,256]{1,0:T(8,128)S(1)} %stage.1.refs_3_.refs_5_.mine.index_mine), channel_id=1, source_target_pairs={{0,1},{1,0},{2,3},{3,2},{4,5},{5,4},{6,7},{7,6},{8,9},{9,8},{10,11... | collective-permute-start | bytes 3170312 | tf_op jit(solution)/shard_map/ppermute | solution.py:158
  3.3 36.4 %collective-permute-start.5 = (f32[1024,256]{1,0:T(8,128)S(1)}, f32[1024,256]{1,0:T(8,128)}, u32[]{:S(2)}, u32[]{:S(2)}) collective-permute-start(f32[1024,256]{1,0:T(8,128)S(1)} %bitcast.6), channel_id=1, source_target_pairs={{0,1},{1,0},{2,3},{3,2},{4,5},{5,4},{6,7},{7,6},{8,9},{9,8},{10,11... | collective-permute-start | bytes 3145736 | tf_op jit(solution)/shard_map/ppermute | solution.py:159
  5.8 10.2 %collective-permute-start = (f32[4,32,256]{2,1,0:T(8,128)S(1)}, f32[4,32,256]{2,1,0:T(8,128)S(1)}, u32[]{:S(2)}, u32[]{:S(2)}) collective-permute-start(f32[4,32,256]{2,1,0:T(8,128)S(1)} %dynamic-slice_bitcast_fusion.refs_1_), channel_id=1, source_target_pairs={{8,16},{24,32},{40,48},{56,64},{72,80},{88,96},{104,112},{120,128}... | collective-permute-start | bytes 393224 | tf_op jit(solution)/shard_map/ppermute | solution.py:134
  12.4 6.9 %collective-permute-start.1 = (f32[4,32,256]{2,1,0:T(8,128)S(1)}, f32[4,32,256]{2,1,0:T(8,128)S(1)}, u32[]{:S(2)}, u32[]{:S(2)}) collective-permute-start(f32[4,32,256]{2,1,0:T(8,128)S(1)} %dynamic-slice_bitcast_fusion.refs_1_), channel_id=1, source_target_pairs={{0,8},{16,24},{32,40},{48,56},{64,72},{80,88},{96,104},{112,120},{... | collective-permute-start | bytes 393224 | tf_op jit(solution)/shard_map/ppermute | solution.py:134
  32.6 11.2 %collective-permute-start.3 = (f32[4,32,256]{2,1,0:T(8,128)S(1)}, f32[4,32,256]{2,1,0:T(8,128)S(1)}, u32[]{:S(2)}, u32[]{:S(2)}) collective-permute-start(f32[4,32,256]{2,1,0:T(8,128)S(1)} %shard_map.74.refs_1_), channel_id=1, source_target_pairs={{8,16},{24,32},{40,48},{56,64},{72,80},{88,96},{104,112},{120,128}... | collective-permute-start | bytes 393224 | tf_op jit(solution)/shard_map/ppermute | solution.py:134
  37.8 6.9 %collective-permute-start.4 = (f32[4,32,256]{2,1,0:T(8,128)S(1)}, f32[4,32,256]{2,1,0:T(8,128)S(1)}, u32[]{:S(2)}, u32[]{:S(2)}) collective-permute-start(f32[4,32,256]{2,1,0:T(8,128)S(1)} %shard_map.74.refs_1_), channel_id=1, source_target_pairs={{0,8},{16,24},{32,40},{48,56},{64,72},{80,88},{96,104},{112,120},{... | collective-permute-start | bytes 393224 | tf_op jit(solution)/shard_map/ppermute | solution.py:134
  58.5 10.7 %collective-permute-start.6 = (f32[4,32,256]{2,1,0:T(8,128)S(1)}, f32[4,32,256]{2,1,0:T(8,128)S(1)}, u32[]{:S(2)}, u32[]{:S(2)}) collective-permute-start(f32[4,32,256]{2,1,0:T(8,128)S(1)} %get-tuple-element.13), channel_id=1, source_target_pairs={{8,16},{24,32},{40,48},{56,64},{72,80},{88,96},{104,112},{120,128}... | collective-permute-start | bytes 393224 | tf_op jit(solution)/shard_map/ppermute | solution.py:134
  64.2 6.9 %collective-permute-start.7 = (f32[4,32,256]{2,1,0:T(8,128)S(1)}, f32[4,32,256]{2,1,0:T(8,128)S(1)}, u32[]{:S(2)}, u32[]{:S(2)}) collective-permute-start(f32[4,32,256]{2,1,0:T(8,128)S(1)} %get-tuple-element.14), channel_id=1, source_target_pairs={{0,8},{16,24},{32,40},{48,56},{64,72},{80,88},{96,104},{112,120},{... | collective-permute-start | bytes 393224 | tf_op jit(solution)/shard_map/ppermute | solution.py:134

commit v4 on v3

--- a/solution.py
+++ b/solution.py
@@ -16,13 +16,20 @@
     return high, low
 
 
-def product(x, block, dims):
+def product(x, high, low, dims):
     m = x.shape[0]
     xh, xl = split(x)
-    bh, bl = split(block)
     dot = lambda a, b: lax.dot_general(a, b, (dims, ((), ())), preferred_element_type=jnp.float32)
-    both = dot(jnp.concatenate([xh, xl], axis=0), bh)
-    return both[:m] + (both[m:] + dot(xh, bl))
+    both = dot(jnp.concatenate([xh, xl], axis=0), high)
+    return both[:m] + (both[m:] + dot(xh, low))
+
+
+def index_tile(index, line):
+    return jnp.broadcast_to(index[pl.ds(1024 + line, 1), :], (8, 256))[None]
+
+
+def swapped(thirds):
+    return thirds[2 * HB :] + thirds[HB : 2 * HB] + thirds[:HB]
 
 
 def pick(fields, index):
@@ -32,33 +39,49 @@
     return picked
 
 
-def forward_kernel(row, low, own, high, mine, theirs, index_mine, index_theirs, out):
+def split_kernel(*refs):
+    count = len(refs) // 3
+    for block, high, low in zip(refs[:count], refs[count::2], refs[count + 1 :: 2]):
+        for i in range(HB):
+            rows = pl.ds(i * 256, 256)
+            high[rows, :], low[rows, :] = split(block[rows, :])
+
+
+def forward_kernel(line, parts, first, own, second, index_mine, index_theirs, *refs):
+    *blocks, out = refs
     n = own.shape[1]
-    fields = [ref[j] for ref in (low, own, high) for j in range(HB)]
-    turned = fields[2 * HB :] + fields[HB : 2 * HB] + fields[:HB]
+    fields = [ref[j].reshape(n // 8, 8, 256) for ref in (first, own, second) for j in range(HB)]
     for i in range(HB):
+        rows = pl.ds(i * 256, 256)
         total = None
-        for blocks, index, window in ((mine, index_mine, fields), (theirs, index_theirs, turned)):
-            where = jnp.broadcast_to(index[pl.ds(index.shape[0] - 8 + row + i, 1), :], (n, 256))
-            part = product(pick(window, where), blocks[pl.ds(i * 256, 256), :], ((1,), (1,)))
+        for s, (index, window) in enumerate(((index_mine, fields), (index_theirs, swapped(fields)))):
+            high, low = (blocks[2 * s][rows, :], blocks[2 * s + 1][rows, :]) if parts else split(blocks[s][rows, :])
+            part = product(pick(window, index_tile(index, line + i)).reshape(n, 256), high, low, ((1,), (1,)))
             total = part if total is None else total + part
         for x in range(out.shape[0]):
             out[x, i] = total
 
 
-def backward_kernel(parts, mine, theirs, index_mine, index_theirs, low, own, high):
+def backward_kernel(parts, index_mine, index_theirs, mine_high, mine_low, theirs_high, theirs_low, first, own, second):
     n = own.shape[1]
-    outs = [(ref, j) for ref in (low, own, high) for j in range(HB)]
-    turned = outs[2 * HB :] + outs[HB : 2 * HB] + outs[:HB]
-    for ref, j in outs:
-        ref[j] = jnp.zeros((n, 256), jnp.float32)
+    mine, theirs = [], []
     for i in range(HB):
+        rows = pl.ds(i * 256, 256)
         side = (parts[0, i] + parts[1, i]) + (parts[2, i] + parts[3, i])
-        for blocks, index, window in ((mine, index_mine, outs), (theirs, index_theirs, turned)):
-            where = jnp.broadcast_to(index[pl.ds(index.shape[0] - 8 + i, 1), :], (n, 256))
-            term = product(side, blocks[pl.ds(i * 256, 256), :], ((1,), (0,)))
-            for w, (ref, j) in enumerate(window):
-                ref[j] = ref[j] + jnp.where(where == w, term, 0.0)
+        for terms, index, high, low in (
+            (mine, index_mine, mine_high, mine_low),
+            (theirs, index_theirs, theirs_high, theirs_low),
+        ):
+            term = product(side, high[rows, :], low[rows, :], ((1,), (0,)))
+            terms.append((index_tile(index, i), term.reshape(n // 8, 8, 256)))
+    outs = [(ref, j) for ref in (first, own, second) for j in range(HB)]
+    order = swapped(list(range(3 * HB)))
+    for w, (ref, j) in enumerate(outs):
+        total = jnp.zeros((n // 8, 8, 256), jnp.float32)
+        for terms, place in ((mine, w), (theirs, order[w])):
+            for index, term in terms:
+                total = total + jnp.where(index == place, term, 0.0)
+        ref[j] = total.reshape(n, 256)
 
 
 def fold_kernel(parts, out):
@@ -150,7 +173,7 @@
         compiler_params=pltpu.CompilerParams(vmem_limit_bytes=4 << 20),
         name="stage",
     )(*(pltpu.with_memory_space_constraint(a, pltpu.HBM) for a in operands))
-    mine, panel = lax.optimization_barrier((mine, panel))
+    mine, panel, h = lax.optimization_barrier((mine, panel, h))
 
     swap = [(0, 1), (1, 0)]
     x = lax.dynamic_slice_in_dim(jnp.swapaxes(panel, 1, 2), q * 32, 32, axis=1)
@@ -158,18 +181,21 @@
     theirs = lax.ppermute(mine, "core", swap)
     h_theirs = lax.ppermute(h, "core", swap)
 
-    def forward(line, first, own, second, blocks, other):
-        body = lambda *refs: forward_kernel(line, *refs)
-        parts = call(body, f32(4, HB, 32, 256), 7, 1 << 28, 1 << 22)(first, own, second, blocks, other, mine, theirs)
+    def forward(line, first, own, second, blocks):
+        body = lambda *refs: forward_kernel(line, len(blocks) == 4, *refs)
+        operands = (first, own, second, mine, theirs, *blocks)
+        parts = call(body, f32(4, HB, 32, 256), len(operands), 1 << 28, 1 << 22)(*operands)
         return lax.all_to_all(parts, "x", 0, 0, tiled=True)
 
-    mid = forward(0, x_first, x, x_second, mine, theirs)
+    mid = forward(0, x_first, x, x_second, (mine, theirs))
     mid = call(fold_kernel, f32(HB, 32, 256), 1, 1 << 18, 1 << 19)(mid)
     mid_first, mid_second = neighbours(mid, mid)
-    side = forward(4, mid_first, mid, mid_second, h, h_theirs)
+    half = jax.ShapeDtypeStruct((1024, 256), jnp.bfloat16)
+    parts = call(split_kernel, (half,) * 8, 4, 1 << 20, 1 << 23)(h, h_theirs, mine, theirs)
+    side = forward(4, mid_first, mid, mid_second, parts[:4])
     shape = f32(HB, 32, 256)
-    first, own, second = call(backward_kernel, (shape, shape, shape), 5, 1 << 28, 1 << 22)(
-        side, mine, theirs, mine, theirs
+    first, own, second = call(backward_kernel, (shape, shape, shape), 7, 1 << 28, 1 << 22)(
+        side, mine, theirs, *parts[4:]
     )
     first, second = neighbours(first, second)
     packed = call(pack_kernel, f32(8, 32, 128), 3, 1 << 20, 1 << 20)(own, first, second)

time: 81 us -> 79.5 us (0.981)
  the two profiles are of different devices: /device:TPU:768 before, /device:TPU:16 now
where the time goes in v4:
time: 79.5 us; the launch traced here: 79 us
  starting transfers between devices  34.6 us (44%)
  blocking collectives  29.5 us (37%)
  waiting for transfers between devices  8.53 us (11%)
  Pallas kernels  6.29 us (8%)
    ppermute x6, starting transfers between devices, neighbours(): lax.ppermute(field, ('rows', 'core'), pairs + [(b, a) for a, b in pairs])  30.2 us
    all_to_all x2, blocking collectives, forward(): return lax.all_to_all(parts, 'x', 0, 0, tiled=True)  21 us
    ppermute x6, waiting for transfers between devices, neighbours(): lax.ppermute(field, ('rows', 'core'), pairs + [(b, a) for a, b in pairs])  8.53 us
    all_to_all x1, blocking collectives, steps(): arrived = lax.all_to_all(packed, ('x', 'core'), 0, 0, tiled=True)  8.49 us
    ppermute x1, starting transfers between devices, steps(): h_theirs = lax.ppermute(h, 'core', swap)  2.41 us
    ppermute x1, starting transfers between devices, steps(): theirs = lax.ppermute(mine, 'core', swap)  1.92 us
    pallas_call x1, Pallas kernels, steps(): call(split_kernel, (half,) * 8, 4, 1 << 20, 1 << 23)  1.89 us
  transfers between devices with their start and end apart: 8, of which 4 were waited for; matrix products, arithmetic and copies ran while one was open for 0% of the time, Pallas kernels for 3%

profile of v4, /device:TPU:16, one launch (start us, length us, event | category | flops | bytes accessed | tf_op | source)
XLA Modules:
  0.0 79.0 jit_solution(18060695924955562436)
XLA Ops:
  0.0 0.0 copy-start
  0.0 0.0 copy-start.1
  0.0 1.4 %stage.1.refs_3_.refs_5_.refs_2_.index_mine = f32[1032,256]{1,0:T(8,128)S(1)} custom-call(s32[4]{0:T(128)} %bitcast.9, s32[4]{0:T(128)} %refs_1_.1, s32[4]{0:T(128)} %bitcast.10, s32[4]{0:T(128)} %refs_3_.1, f32[1024,256]{1,0:T(8,128)} %bitcast.8), custom_call_target="tpu_custom_call" | custom-call | tf_op jit(solution)/shard_map/stage/pallas_call | solution.py:167
  1.4 1.9 %collective-permute-start.2 = (f32[1032,256]{1,0:T(8,128)S(1)}, f32[1032,256]{1,0:T(8,128)S(1)}, u32[]{:S(2)}, u32[]{:S(2)}) collective-permute-start(f32[1032,256]{1,0:T(8,128)S(1)} %stage.1.refs_3_.refs_5_.refs_2_.index_mine), channel_id=1, source_target_pairs={{0,1},{1,0},{2,3},{3,2},{4,5},{5,4},{6,7},{7,6},{8,9},{9,8},{10,11... | collective-permute-start | bytes 3170312 | tf_op jit(solution)/shard_map/ppermute | solution.py:181
  3.3 0.0 copy-done.1
  3.3 2.4 %collective-permute-start.5 = (f32[1024,256]{1,0:T(8,128)S(1)}, f32[1024,256]{1,0:T(8,128)}, u32[]{:S(2)}, u32[]{:S(2)}) collective-permute-start(f32[1024,256]{1,0:T(8,128)S(1)} %bitcast.6), channel_id=1, source_target_pairs={{0,1},{1,0},{2,3},{3,2},{4,5},{5,4},{6,7},{7,6},{8,9},{9,8},{10,11... | collective-permute-start | bytes 3145736 | tf_op jit(solution)/shard_map/ppermute | solution.py:182
  5.7 0.0 copy-done
  5.8 3.5 %collective-permute-start.1 = (f32[4,32,256]{2,1,0:T(8,128)S(1)}, f32[4,32,256]{2,1,0:T(8,128)S(1)}, u32[]{:S(2)}, u32[]{:S(2)}) collective-permute-start(f32[4,32,256]{2,1,0:T(8,128)S(1)} %dynamic-slice_bitcast_fusion.refs_1_), channel_id=1, source_target_pairs={{0,8},{16,24},{32,40},{48,56},{64,72},{80,88},{96,104},{112,120},{... | collective-permute-start | bytes 393224 | tf_op jit(solution)/shard_map/ppermute | solution.py:157
  9.3 13.9 %collective-permute-start = (f32[4,32,256]{2,1,0:T(8,128)S(1)}, f32[4,32,256]{2,1,0:T(8,128)S(1)}, u32[]{:S(2)}, u32[]{:S(2)}) collective-permute-start(f32[4,32,256]{2,1,0:T(8,128)S(1)} %dynamic-slice_bitcast_fusion.refs_1_), channel_id=1, source_target_pairs={{8,16},{24,32},{40,48},{56,64},{72,80},{88,96},{104,112},{120,128}... | collective-permute-start | bytes 393224 | tf_op jit(solution)/shard_map/ppermute | solution.py:157
  23.1 0.0 collective-permute-done.1.refs_2_
  23.1 2.9 %collective-permute-done.refs_0_ = f32[4,32,256]{2,1,0:T(8,128)S(1)} collective-permute-done((f32[4,32,256]{2,1,0:T(8,128)S(1)}, f32[4,32,256]{2,1,0:T(8,128)S(1)}, u32[]{:S(2)}, u32[]{:S(2)}) %collective-permute-start) | collective-permute-done | bytes 131104 | tf_op jit(solution)/shard_map/ppermute | solution.py:157
  26.1 0.0 collective-permute-done.2.refs_4_.refs_6_.refs_3_.index_theirs
  26.1 0.8 shard_map.73
  26.9 10.5 %all_to_all.15.parts = f32[4,4,32,256]{3,2,1,0:T(8,128)S(1)} all-to-all(f32[4,4,32,256]{3,2,1,0:T(8,128)S(1)} %shard_map.73), channel_id=1, replica_groups=mesh['rows'=128,'x'=4,'core'=2] {'x'}, dimensions={0} | all-to-all | bytes 1048576 | tf_op jit(solution)/shard_map/all_to_all | solution.py:188
  37.4 1.9 %collective-permute-start.4 = (f32[4,32,256]{2,1,0:T(8,128)S(1)}, f32[4,32,256]{2,1,0:T(8,128)S(1)}, u32[]{:S(2)}, u32[]{:S(2)}) collective-permute-start(f32[4,32,256]{2,1,0:T(8,128)S(1)} %shard_map.74.refs_1_), channel_id=1, source_target_pairs={{0,8},{16,24},{32,40},{48,56},{64,72},{80,88},{96,104},{112,120},{... | collective-permute-start | bytes 393224 | tf_op jit(solution)/shard_map/ppermute | solution.py:157
  39.3 4.8 %collective-permute-start.3 = (f32[4,32,256]{2,1,0:T(8,128)S(1)}, f32[4,32,256]{2,1,0:T(8,128)S(1)}, u32[]{:S(2)}, u32[]{:S(2)}) collective-permute-start(f32[4,32,256]{2,1,0:T(8,128)S(1)} %shard_map.74.refs_1_), channel_id=1, source_target_pairs={{8,16},{24,32},{40,48},{56,64},{72,80},{88,96},{104,112},{120,128}... | collective-permute-start | bytes 393224 | tf_op jit(solution)/shard_map/ppermute | solution.py:157
  44.1 0.0 collective-permute-done.5.refs_1_
  44.1 1.9 %shard_map.75 = (bf16[1024,256]{1,0:T(8,128)(2,1)S(1)}, bf16[1024,256]{1,0:T(8,128)(2,1)S(1)}, bf16[1024,256]{1,0:T(8,128)(2,1)S(1)}, bf16[1024,256]{1,0:T(8,128...) custom-call(f32[1024,256]{1,0:T(8,128)S(1)} %bitcast.7, ...), custom_call_target="tpu_custom_call" | custom-call | flops 1048576 | bytes 8388608 | tf_op jit(solution)/shard_map/pallas_call | solution.py:194
  46.0 0.0 collective-permute-done.4.refs_2_
  46.0 1.0 %collective-permute-done.3.refs_0_ = f32[4,32,256]{2,1,0:T(8,128)S(1)} collective-permute-done((f32[4,32,256]{2,1,0:T(8,128)S(1)}, f32[4,32,256]{2,1,0:T(8,128)S(1)}, u32[]{:S(2)}, u32[]{:S(2)}) %collective-permute-start.3) | collective-permute-done | bytes 131104 | tf_op jit(solution)/shard_map/ppermute | solution.py:157
  47.0 0.7 shard_map.76
  47.8 10.5 %all_to_all.16.parts = f32[4,4,32,256]{3,2,1,0:T(8,128)S(1)} all-to-all(f32[4,4,32,256]{3,2,1,0:T(8,128)S(1)} %shard_map.76), channel_id=1, replica_groups=mesh['rows'=128,'x'=4,'core'=2] {'x'}, dimensions={0} | all-to-all | bytes 1048576 | tf_op jit(solution)/shard_map/all_to_all | solution.py:188
  58.3 0.6 shard_map.77
  58.8 3.9 %collective-permute-start.6 = (f32[4,32,256]{2,1,0:T(8,128)S(1)}, f32[4,32,256]{2,1,0:T(8,128)S(1)}, u32[]{:S(2)}, u32[]{:S(2)}) collective-permute-start(f32[4,32,256]{2,1,0:T(8,128)S(1)} %get-tuple-element.31), channel_id=1, source_target_pairs={{8,16},{24,32},{40,48},{56,64},{72,80},{88,96},{104,112},{120,128}... | collective-permute-start | bytes 393224 | tf_op jit(solution)/shard_map/ppermute | solution.py:157
  62.8 2.3 %collective-permute-start.7 = (f32[4,32,256]{2,1,0:T(8,128)S(1)}, f32[4,32,256]{2,1,0:T(8,128)S(1)}, u32[]{:S(2)}, u32[]{:S(2)}) collective-permute-start(f32[4,32,256]{2,1,0:T(8,128)S(1)} %get-tuple-element.32), channel_id=1, source_target_pairs={{0,8},{16,24},{32,40},{48,56},{64,72},{80,88},{96,104},{112,120},{... | collective-permute-start | bytes 393224 | tf_op jit(solution)/shard_map/ppermute | solution.py:157
  65.0 0.7 collective-permute-done.6.below
  65.7 3.9 %collective-permute-done.7.above = f32[4,32,256]{2,1,0:T(8,128)S(1)} collective-permute-done((f32[4,32,256]{2,1,0:T(8,128)S(1)}, f32[4,32,256]{2,1,0:T(8,128)S(1)}, u32[]{:S(2)}, u32[]{:S(2)}) %collective-permute-start.7) | collective-permute-done | bytes 131104 | tf_op jit(solution)/shard_map/ppermute | solution.py:157
  69.6 0.2 shard_map.78
  69.8 8.5 %all_to_all.17.parts = f32[8,32,128]{2,1,0:T(8,128)S(1)} all-to-all(f32[8,32,128]{2,1,0:T(8,128)S(1)} %shard_map.78), channel_id=1, replica_groups=mesh['rows'=128,'x'=4,'core'=2] {'x','core'}, dimensions={0} | all-to-all | bytes 262144 | tf_op jit(solution)/shard_map/all_to_all | solution.py:202
  78.3 0.7 shard_map.79
  (2 shorter events, 0.0 us)
Async XLA Ops:
  0.0 5.7 %copy-start = (f32[4,256,64]{1,2,0:T(8,128)S(1)}, f32[4,256,64]{1,2,0:T(8,128)}, u32[]{:S(2)}) copy-start(f32[4,256,64]{1,2,0:T(8,128)} %param.13) | copy-start | bytes 786436
  0.0 3.3 %copy-start.1 = (f32[4,1,256,256]{3,2,1,0:T(8,128)S(1)}, f32[4,1,256,256]{3,2,1,0:T(8,128)}, u32[]{:S(2)}) copy-start(f32[4,1,256,256]{3,2,1,0:T(8,128)} %param.10) | copy-start | bytes 3145732
  1.4 24.7 %collective-permute-start.2 = (f32[1032,256]{1,0:T(8,128)S(1)}, f32[1032,256]{1,0:T(8,128)S(1)}, u32[]{:S(2)}, u32[]{:S(2)}) collective-permute-start(f32[1032,256]{1,0:T(8,128)S(1)} %stage.1.refs_3_.refs_5_.refs_2_.index_mine), channel_id=1, source_target_pairs={{0,1},{1,0},{2,3},{3,2},{4,5},{5,4},{6,7},{7,6},{8,9},{9,8},{10,11... | collective-permute-start | bytes 3170312 | tf_op jit(solution)/shard_map/ppermute | solution.py:181
  3.3 40.8 %collective-permute-start.5 = (f32[1024,256]{1,0:T(8,128)S(1)}, f32[1024,256]{1,0:T(8,128)}, u32[]{:S(2)}, u32[]{:S(2)}) collective-permute-start(f32[1024,256]{1,0:T(8,128)S(1)} %bitcast.6), channel_id=1, source_target_pairs={{0,1},{1,0},{2,3},{3,2},{4,5},{5,4},{6,7},{7,6},{8,9},{9,8},{10,11... | collective-permute-start | bytes 3145736 | tf_op jit(solution)/shard_map/ppermute | solution.py:182
  5.8 17.4 %collective-permute-start.1 = (f32[4,32,256]{2,1,0:T(8,128)S(1)}, f32[4,32,256]{2,1,0:T(8,128)S(1)}, u32[]{:S(2)}, u32[]{:S(2)}) collective-permute-start(f32[4,32,256]{2,1,0:T(8,128)S(1)} %dynamic-slice_bitcast_fusion.refs_1_), channel_id=1, source_target_pairs={{0,8},{16,24},{32,40},{48,56},{64,72},{80,88},{96,104},{112,120},{... | collective-permute-start | bytes 393224 | tf_op jit(solution)/shard_map/ppermute | solution.py:157
  9.3 16.8 %collective-permute-start = (f32[4,32,256]{2,1,0:T(8,128)S(1)}, f32[4,32,256]{2,1,0:T(8,128)S(1)}, u32[]{:S(2)}, u32[]{:S(2)}) collective-permute-start(f32[4,32,256]{2,1,0:T(8,128)S(1)} %dynamic-slice_bitcast_fusion.refs_1_), channel_id=1, source_target_pairs={{8,16},{24,32},{40,48},{56,64},{72,80},{88,96},{104,112},{120,128}... | collective-permute-start | bytes 393224 | tf_op jit(solution)/shard_map/ppermute | solution.py:157
  37.4 8.6 %collective-permute-start.4 = (f32[4,32,256]{2,1,0:T(8,128)S(1)}, f32[4,32,256]{2,1,0:T(8,128)S(1)}, u32[]{:S(2)}, u32[]{:S(2)}) collective-permute-start(f32[4,32,256]{2,1,0:T(8,128)S(1)} %shard_map.74.refs_1_), channel_id=1, source_target_pairs={{0,8},{16,24},{32,40},{48,56},{64,72},{80,88},{96,104},{112,120},{... | collective-permute-start | bytes 393224 | tf_op jit(solution)/shard_map/ppermute | solution.py:157
  39.3 7.7 %collective-permute-start.3 = (f32[4,32,256]{2,1,0:T(8,128)S(1)}, f32[4,32,256]{2,1,0:T(8,128)S(1)}, u32[]{:S(2)}, u32[]{:S(2)}) collective-permute-start(f32[4,32,256]{2,1,0:T(8,128)S(1)} %shard_map.74.refs_1_), channel_id=1, source_target_pairs={{8,16},{24,32},{40,48},{56,64},{72,80},{88,96},{104,112},{120,128}... | collective-permute-start | bytes 393224 | tf_op jit(solution)/shard_map/ppermute | solution.py:157
  58.8 6.9 %collective-permute-start.6 = (f32[4,32,256]{2,1,0:T(8,128)S(1)}, f32[4,32,256]{2,1,0:T(8,128)S(1)}, u32[]{:S(2)}, u32[]{:S(2)}) collective-permute-start(f32[4,32,256]{2,1,0:T(8,128)S(1)} %get-tuple-element.31), channel_id=1, source_target_pairs={{8,16},{24,32},{40,48},{56,64},{72,80},{88,96},{104,112},{120,128}... | collective-permute-start | bytes 393224 | tf_op jit(solution)/shard_map/ppermute | solution.py:157
  62.8 6.9 %collective-permute-start.7 = (f32[4,32,256]{2,1,0:T(8,128)S(1)}, f32[4,32,256]{2,1,0:T(8,128)S(1)}, u32[]{:S(2)}, u32[]{:S(2)}) collective-permute-start(f32[4,32,256]{2,1,0:T(8,128)S(1)} %get-tuple-element.32), channel_id=1, source_target_pairs={{0,8},{16,24},{32,40},{48,56},{64,72},{80,88},{96,104},{112,120},{... | collective-permute-start | bytes 393224 | tf_op jit(solution)/shard_map/ppermute | solution.py:157

commit v5 on v4

--- a/solution.py
+++ b/solution.py
@@ -84,8 +84,8 @@
         ref[j] = total.reshape(n, 256)
 
 
-def fold_kernel(parts, out):
-    out[...] = (parts[0] + parts[1]) + (parts[2] + parts[3])
+def fold_kernel(own, second, first, third, out):
+    out[...] = (own[...] + first[...]) + (second[...] + third[...])
 
 
 def stage_kernel(*refs):
@@ -181,18 +181,20 @@
     theirs = lax.ppermute(mine, "core", swap)
     h_theirs = lax.ppermute(h, "core", swap)
 
-    def forward(line, first, own, second, blocks):
+    def forward(line, first, own, second, blocks, copies):
         body = lambda *refs: forward_kernel(line, len(blocks) == 4, *refs)
         operands = (first, own, second, mine, theirs, *blocks)
-        parts = call(body, f32(4, HB, 32, 256), len(operands), 1 << 28, 1 << 22)(*operands)
-        return lax.all_to_all(parts, "x", 0, 0, tiled=True)
-
-    mid = forward(0, x_first, x, x_second, (mine, theirs))
-    mid = call(fold_kernel, f32(HB, 32, 256), 1, 1 << 18, 1 << 19)(mid)
+        return call(body, f32(copies, HB, 32, 256), len(operands), 1 << 28, 1 << 22)(*operands)
+
+    mids = [forward(0, x_first, x, x_second, (mine, theirs), 1).reshape(HB, 32, 256)]
+    for step in (2, 1, 3):
+        mids.append(lax.ppermute(mids[0], "x", [(i, i ^ step) for i in range(4)]))
+    mid = call(fold_kernel, f32(HB, 32, 256), 4, 1 << 18, 1 << 19)(*mids)
     mid_first, mid_second = neighbours(mid, mid)
     half = jax.ShapeDtypeStruct((1024, 256), jnp.bfloat16)
     parts = call(split_kernel, (half,) * 8, 4, 1 << 20, 1 << 23)(h, h_theirs, mine, theirs)
-    side = forward(4, mid_first, mid, mid_second, parts[:4])
+    side = forward(4, mid_first, mid, mid_second, parts[:4], 4)
+    side = lax.all_to_all(side, "x", 0, 0, tiled=True)
     shape = f32(HB, 32, 256)
     first, own, second = call(backward_kernel, (shape, shape, shape), 7, 1 << 28, 1 << 22)(
         side, mine, theirs, *parts[4:]

time: 79.5 us -> 83.9 us (1.055)
  the two profiles are of different devices: /device:TPU:16 before, /device:TPU:32 now
where the time goes in v5:
time: 83.9 us; the launch traced here: 83.3 us
  starting transfers between devices  39.1 us (47%)
  blocking collectives  21.2 us (25%)
  waiting for transfers between devices  16.6 us (20%)
  Pallas kernels  6.27 us (7%)
    ppermute x6, starting transfers between devices, neighbours(): lax.ppermute(field, ('rows', 'core'), pairs + [(b, a) for a, b in pairs])  24.3 us
    all_to_all x1, blocking collectives, steps(): side = lax.all_to_all(side, 'x', 0, 0, tiled=True)  12.7 us
    ppermute x6, waiting for transfers between devices, neighbours(): lax.ppermute(field, ('rows', 'core'), pairs + [(b, a) for a, b in pairs])  11.9 us
    ppermute x3, starting transfers between devices, steps(): mids.append(lax.ppermute(mids[0], 'x', [(i, i ^ step) for i in range(4)]))  10.4 us
    all_to_all x1, blocking collectives, steps(): arrived = lax.all_to_all(packed, ('x', 'core'), 0, 0, tiled=True)  8.49 us
    ppermute x3, waiting for transfers between devices, steps(): mids.append(lax.ppermute(mids[0], 'x', [(i, i ^ step) for i in range(4)]))  4.72 us
    ppermute x1, starting transfers between devices, steps(): h_theirs = lax.ppermute(h, 'core', swap)  2.41 us
    ppermute x1, starting transfers between devices, steps(): theirs = lax.ppermute(mine, 'core', swap)  1.92 us
  transfers between devices with their start and end apart: 11, of which 7 were waited for; matrix products, arithmetic and copies ran while one was open for 0% of the time, Pallas kernels for 3%

profile of v5, /device:TPU:32, one launch (start us, length us, event | category | flops | bytes accessed | tf_op | source)
XLA Modules:
  0.0 83.3 jit_solution(11308243534061093768)
XLA Ops:
  0.0 0.0 copy-start
  0.0 0.0 copy-start.1
  0.0 1.4 %stage.1.refs_3_.refs_5_.refs_2_.index_mine = f32[1032,256]{1,0:T(8,128)S(1)} custom-call(s32[4]{0:T(128)} %bitcast.14, s32[4]{0:T(128)} %refs_1_.1, s32[4]{0:T(128)} %bitcast.15, s32[4]{0:T(128)} %refs_3_.1, f32[1024,256]{1,0:T(8,128)} %bitcast.13), custom_call_target="tpu_custom_call" | custom-call | tf_op jit(solution)/shard_map/stage/pallas_call | solution.py:167
  1.4 1.9 %collective-permute-start.2 = (f32[1032,256]{1,0:T(8,128)S(1)}, f32[1032,256]{1,0:T(8,128)S(1)}, u32[]{:S(2)}, u32[]{:S(2)}) collective-permute-start(f32[1032,256]{1,0:T(8,128)S(1)} %stage.1.refs_3_.refs_5_.refs_2_.index_mine), channel_id=1, source_target_pairs={{0,1},{1,0},{2,3},{3,2},{4,5},{5,4},{6,7},{7,6},{8,9},{9,8},{10,11... | collective-permute-start | bytes 3170312 | tf_op jit(solution)/shard_map/ppermute | solution.py:181
  3.3 0.0 copy-done.1
  3.3 2.4 %collective-permute-start.8 = (f32[1024,256]{1,0:T(8,128)S(1)}, f32[1024,256]{1,0:T(8,128)}, u32[]{:S(2)}, u32[]{:S(2)}) collective-permute-start(f32[1024,256]{1,0:T(8,128)S(1)} %bitcast.7), channel_id=1, source_target_pairs={{0,1},{1,0},{2,3},{3,2},{4,5},{5,4},{6,7},{7,6},{8,9},{9,8},{10,11... | collective-permute-start | bytes 3145736 | tf_op jit(solution)/shard_map/ppermute | solution.py:182
  5.7 0.0 copy-done
  5.8 2.6 %collective-permute-start.1 = (f32[4,32,256]{2,1,0:T(8,128)S(1)}, f32[4,32,256]{2,1,0:T(8,128)S(1)}, u32[]{:S(2)}, u32[]{:S(2)}) collective-permute-start(f32[4,32,256]{2,1,0:T(8,128)S(1)} %dynamic-slice_bitcast_fusion.refs_1_), channel_id=1, source_target_pairs={{0,8},{16,24},{32,40},{48,56},{64,72},{80,88},{96,104},{112,120},{... | collective-permute-start | bytes 393224 | tf_op jit(solution)/shard_map/ppermute | solution.py:157
  8.4 2.1 %collective-permute-start = (f32[4,32,256]{2,1,0:T(8,128)S(1)}, f32[4,32,256]{2,1,0:T(8,128)S(1)}, u32[]{:S(2)}, u32[]{:S(2)}) collective-permute-start(f32[4,32,256]{2,1,0:T(8,128)S(1)} %dynamic-slice_bitcast_fusion.refs_1_), channel_id=1, source_target_pairs={{8,16},{24,32},{40,48},{56,64},{72,80},{88,96},{104,112},{120,128}... | collective-permute-start | bytes 393224 | tf_op jit(solution)/shard_map/ppermute | solution.py:157
  10.5 2.4 %collective-permute-done.1.refs_2_ = f32[4,32,256]{2,1,0:T(8,128)S(1)} collective-permute-done((f32[4,32,256]{2,1,0:T(8,128)S(1)}, f32[4,32,256]{2,1,0:T(8,128)S(1)}, u32[]{:S(2)}, u32[]{:S(2)}) %collective-permute-start.1) | collective-permute-done | bytes 131104 | tf_op jit(solution)/shard_map/ppermute | solution.py:157
  12.9 3.5 %collective-permute-done.refs_0_ = f32[4,32,256]{2,1,0:T(8,128)S(1)} collective-permute-done((f32[4,32,256]{2,1,0:T(8,128)S(1)}, f32[4,32,256]{2,1,0:T(8,128)S(1)}, u32[]{:S(2)}, u32[]{:S(2)}) %collective-permute-start) | collective-permute-done | bytes 131104 | tf_op jit(solution)/shard_map/ppermute | solution.py:157
  16.4 0.0 collective-permute-done.2.refs_4_.refs_6_.refs_3_.index_theirs
  16.4 0.8 shard_map.73
  17.2 4.7 %collective-permute-start.5 = (f32[4,32,256]{2,1,0:T(8,128)S(1)}, f32[4,32,256]{2,1,0:T(8,128)S(1)}, u32[]{:S(2)}, u32[]{:S(2)}) collective-permute-start(f32[4,32,256]{2,1,0:T(8,128)S(1)} %bitcast.9), channel_id=1, source_target_pairs={{0,6},{2,4},{4,2},{6,0},{1,7},{3,5},{5,3},{7,1},{8,14},{10,12},{12... | collective-permute-start | bytes 393224 | tf_op jit(solution)/shard_map/ppermute | solution.py:191
  21.9 2.1 %collective-permute-start.4 = (f32[4,32,256]{2,1,0:T(8,128)S(1)}, f32[4,32,256]{2,1,0:T(8,128)S(1)}, u32[]{:S(2)}, u32[]{:S(2)}) collective-permute-start(f32[4,32,256]{2,1,0:T(8,128)S(1)} %bitcast.10), channel_id=1, source_target_pairs={{0,2},{2,0},{4,6},{6,4},{1,3},{3,1},{5,7},{7,5},{8,10},{10,8},{12,... | collective-permute-start | bytes 393224 | tf_op jit(solution)/shard_map/ppermute | solution.py:191
  24.0 3.6 %collective-permute-start.3 = (f32[4,32,256]{2,1,0:T(8,128)S(1)}, f32[4,32,256]{2,1,0:T(8,128)S(1)}, u32[]{:S(2)}, u32[]{:S(2)}) collective-permute-start(f32[4,32,256]{2,1,0:T(8,128)S(1)} %bitcast.11), channel_id=1, source_target_pairs={{0,4},{2,6},{4,0},{6,2},{1,5},{3,7},{5,1},{7,3},{8,12},{10,14},{12... | collective-permute-start | bytes 393224 | tf_op jit(solution)/shard_map/ppermute | solution.py:191
  27.7 0.0 collective-permute-done.5.third
  27.7 1.1 %collective-permute-done.4.first = f32[4,32,256]{2,1,0:T(8,128)S(1)} collective-permute-done((f32[4,32,256]{2,1,0:T(8,128)S(1)}, f32[4,32,256]{2,1,0:T(8,128)S(1)}, u32[]{:S(2)}, u32[]{:S(2)}) %collective-permute-start.4) | collective-permute-done | bytes 131104 | tf_op jit(solution)/shard_map/ppermute | solution.py:191
  28.8 3.6 %collective-permute-done.3.second = f32[4,32,256]{2,1,0:T(8,128)S(1)} collective-permute-done((f32[4,32,256]{2,1,0:T(8,128)S(1)}, f32[4,32,256]{2,1,0:T(8,128)S(1)}, u32[]{:S(2)}, u32[]{:S(2)}) %collective-permute-start.3) | collective-permute-done | bytes 131104 | tf_op jit(solution)/shard_map/ppermute | solution.py:191
  32.4 2.0 %collective-permute-start.7 = (f32[4,32,256]{2,1,0:T(8,128)S(1)}, f32[4,32,256]{2,1,0:T(8,128)S(1)}, u32[]{:S(2)}, u32[]{:S(2)}) collective-permute-start(f32[4,32,256]{2,1,0:T(8,128)S(1)} %shard_map.74.refs_1_), channel_id=1, source_target_pairs={{0,8},{16,24},{32,40},{48,56},{64,72},{80,88},{96,104},{112,120},{... | collective-permute-start | bytes 393224 | tf_op jit(solution)/shard_map/ppermute | solution.py:157
  34.5 10.5 %collective-permute-start.6 = (f32[4,32,256]{2,1,0:T(8,128)S(1)}, f32[4,32,256]{2,1,0:T(8,128)S(1)}, u32[]{:S(2)}, u32[]{:S(2)}) collective-permute-start(f32[4,32,256]{2,1,0:T(8,128)S(1)} %shard_map.74.refs_1_), channel_id=1, source_target_pairs={{8,16},{24,32},{40,48},{56,64},{72,80},{88,96},{104,112},{120,128}... | collective-permute-start | bytes 393224 | tf_op jit(solution)/shard_map/ppermute | solution.py:157
  45.0 0.0 collective-permute-done.8.refs_1_
  45.0 1.9 %shard_map.75 = (bf16[1024,256]{1,0:T(8,128)(2,1)S(1)}, bf16[1024,256]{1,0:T(8,128)(2,1)S(1)}, bf16[1024,256]{1,0:T(8,128)(2,1)S(1)}, bf16[1024,256]{1,0:T(8,128...) custom-call(f32[1024,256]{1,0:T(8,128)S(1)} %bitcast.8, ...), custom_call_target="tpu_custom_call" | custom-call | flops 1048576 | bytes 8388608 | tf_op jit(solution)/shard_map/pallas_call | solution.py:195
  46.9 0.0 collective-permute-done.7.refs_2_
  46.9 1.0 %collective-permute-done.6.refs_0_ = f32[4,32,256]{2,1,0:T(8,128)S(1)} collective-permute-done((f32[4,32,256]{2,1,0:T(8,128)S(1)}, f32[4,32,256]{2,1,0:T(8,128)S(1)}, u32[]{:S(2)}, u32[]{:S(2)}) %collective-permute-start.6) | collective-permute-done | bytes 131104 | tf_op jit(solution)/shard_map/ppermute | solution.py:157
  47.9 0.7 shard_map.76
  48.7 12.7 %all_to_all.10.parts = f32[4,4,32,256]{3,2,1,0:T(8,128)S(1)} all-to-all(f32[4,4,32,256]{3,2,1,0:T(8,128)S(1)} %shard_map.76), channel_id=1, replica_groups=mesh['rows'=128,'x'=4,'core'=2] {'x'}, dimensions={0} | all-to-all | bytes 1048576 | tf_op jit(solution)/shard_map/all_to_all | solution.py:197
  61.3 0.6 shard_map.77
  61.9 5.1 %collective-permute-start.9 = (f32[4,32,256]{2,1,0:T(8,128)S(1)}, f32[4,32,256]{2,1,0:T(8,128)S(1)}, u32[]{:S(2)}, u32[]{:S(2)}) collective-permute-start(f32[4,32,256]{2,1,0:T(8,128)S(1)} %get-tuple-element.31), channel_id=1, source_target_pairs={{8,16},{24,32},{40,48},{56,64},{72,80},{88,96},{104,112},{120,128}... | collective-permute-start | bytes 393224 | tf_op jit(solution)/shard_map/ppermute | solution.py:157
  67.1 1.9 %collective-permute-start.10 = (f32[4,32,256]{2,1,0:T(8,128)S(1)}, f32[4,32,256]{2,1,0:T(8,128)S(1)}, u32[]{:S(2)}, u32[]{:S(2)}) collective-permute-start(f32[4,32,256]{2,1,0:T(8,128)S(1)} %get-tuple-element.32), channel_id=1, source_target_pairs={{0,8},{16,24},{32,40},{48,56},{64,72},{80,88},{96,104},{112,120},{... | collective-permute-start | bytes 393224 | tf_op jit(solution)/shard_map/ppermute | solution.py:157
  69.0 1.0 %collective-permute-done.9.below = f32[4,32,256]{2,1,0:T(8,128)S(1)} collective-permute-done((f32[4,32,256]{2,1,0:T(8,128)S(1)}, f32[4,32,256]{2,1,0:T(8,128)S(1)}, u32[]{:S(2)}, u32[]{:S(2)}) %collective-permute-start.9) | collective-permute-done | bytes 131104 | tf_op jit(solution)/shard_map/ppermute | solution.py:157
  70.0 3.9 %collective-permute-done.10.above = f32[4,32,256]{2,1,0:T(8,128)S(1)} collective-permute-done((f32[4,32,256]{2,1,0:T(8,128)S(1)}, f32[4,32,256]{2,1,0:T(8,128)S(1)}, u32[]{:S(2)}, u32[]{:S(2)}) %collective-permute-start.10) | collective-permute-done | bytes 131104 | tf_op jit(solution)/shard_map/ppermute | solution.py:157
  73.9 0.2 shard_map.78
  74.1 8.5 %all_to_all.11.parts = f32[8,32,128]{2,1,0:T(8,128)S(1)} all-to-all(f32[8,32,128]{2,1,0:T(8,128)S(1)} %shard_map.78), channel_id=1, replica_groups=mesh['rows'=128,'x'=4,'core'=2] {'x','core'}, dimensions={0} | all-to-all | bytes 262144 | tf_op jit(solution)/shard_map/all_to_all | solution.py:204
  82.6 0.7 shard_map.79
  (2 shorter events, 0.0 us)
Async XLA Ops:
  0.0 5.7 %copy-start = (f32[4,256,64]{1,2,0:T(8,128)S(1)}, f32[4,256,64]{1,2,0:T(8,128)}, u32[]{:S(2)}) copy-start(f32[4,256,64]{1,2,0:T(8,128)} %param.13) | copy-start | bytes 786436
  0.0 3.3 %copy-start.1 = (f32[4,1,256,256]{3,2,1,0:T(8,128)S(1)}, f32[4,1,256,256]{3,2,1,0:T(8,128)}, u32[]{:S(2)}) copy-start(f32[4,1,256,256]{3,2,1,0:T(8,128)} %param.10) | copy-start | bytes 3145732
  1.4 15.1 %collective-permute-start.2 = (f32[1032,256]{1,0:T(8,128)S(1)}, f32[1032,256]{1,0:T(8,128)S(1)}, u32[]{:S(2)}, u32[]{:S(2)}) collective-permute-start(f32[1032,256]{1,0:T(8,128)S(1)} %stage.1.refs_3_.refs_5_.refs_2_.index_mine), channel_id=1, source_target_pairs={{0,1},{1,0},{2,3},{3,2},{4,5},{5,4},{6,7},{7,6},{8,9},{9,8},{10,11... | collective-permute-start | bytes 3170312 | tf_op jit(solution)/shard_map/ppermute | solution.py:181
  3.3 41.7 %collective-permute-start.8 = (f32[1024,256]{1,0:T(8,128)S(1)}, f32[1024,256]{1,0:T(8,128)}, u32[]{:S(2)}, u32[]{:S(2)}) collective-permute-start(f32[1024,256]{1,0:T(8,128)S(1)} %bitcast.7), channel_id=1, source_target_pairs={{0,1},{1,0},{2,3},{3,2},{4,5},{5,4},{6,7},{7,6},{8,9},{9,8},{10,11... | collective-permute-start | bytes 3145736 | tf_op jit(solution)/shard_map/ppermute | solution.py:182
  5.8 7.1 %collective-permute-start.1 = (f32[4,32,256]{2,1,0:T(8,128)S(1)}, f32[4,32,256]{2,1,0:T(8,128)S(1)}, u32[]{:S(2)}, u32[]{:S(2)}) collective-permute-start(f32[4,32,256]{2,1,0:T(8,128)S(1)} %dynamic-slice_bitcast_fusion.refs_1_), channel_id=1, source_target_pairs={{0,8},{16,24},{32,40},{48,56},{64,72},{80,88},{96,104},{112,120},{... | collective-permute-start | bytes 393224 | tf_op jit(solution)/shard_map/ppermute | solution.py:157
  8.4 8.1 %collective-permute-start = (f32[4,32,256]{2,1,0:T(8,128)S(1)}, f32[4,32,256]{2,1,0:T(8,128)S(1)}, u32[]{:S(2)}, u32[]{:S(2)}) collective-permute-start(f32[4,32,256]{2,1,0:T(8,128)S(1)} %dynamic-slice_bitcast_fusion.refs_1_), channel_id=1, source_target_pairs={{8,16},{24,32},{40,48},{56,64},{72,80},{88,96},{104,112},{120,128}... | collective-permute-start | bytes 393224 | tf_op jit(solution)/shard_map/ppermute | solution.py:157
  17.2 10.5 %collective-permute-start.5 = (f32[4,32,256]{2,1,0:T(8,128)S(1)}, f32[4,32,256]{2,1,0:T(8,128)S(1)}, u32[]{:S(2)}, u32[]{:S(2)}) collective-permute-start(f32[4,32,256]{2,1,0:T(8,128)S(1)} %bitcast.9), channel_id=1, source_target_pairs={{0,6},{2,4},{4,2},{6,0},{1,7},{3,5},{5,3},{7,1},{8,14},{10,12},{12... | collective-permute-start | bytes 393224 | tf_op jit(solution)/shard_map/ppermute | solution.py:191
  21.9 6.9 %collective-permute-start.4 = (f32[4,32,256]{2,1,0:T(8,128)S(1)}, f32[4,32,256]{2,1,0:T(8,128)S(1)}, u32[]{:S(2)}, u32[]{:S(2)}) collective-permute-start(f32[4,32,256]{2,1,0:T(8,128)S(1)} %bitcast.10), channel_id=1, source_target_pairs={{0,2},{2,0},{4,6},{6,4},{1,3},{3,1},{5,7},{7,5},{8,10},{10,8},{12,... | collective-permute-start | bytes 393224 | tf_op jit(solution)/shard_map/ppermute | solution.py:191
  24.0 8.4 %collective-permute-start.3 = (f32[4,32,256]{2,1,0:T(8,128)S(1)}, f32[4,32,256]{2,1,0:T(8,128)S(1)}, u32[]{:S(2)}, u32[]{:S(2)}) collective-permute-start(f32[4,32,256]{2,1,0:T(8,128)S(1)} %bitcast.11), channel_id=1, source_target_pairs={{0,4},{2,6},{4,0},{6,2},{1,5},{3,7},{5,1},{7,3},{8,12},{10,14},{12... | collective-permute-start | bytes 393224 | tf_op jit(solution)/shard_map/ppermute | solution.py:191
  32.4 14.5 %collective-permute-start.7 = (f32[4,32,256]{2,1,0:T(8,128)S(1)}, f32[4,32,256]{2,1,0:T(8,128)S(1)}, u32[]{:S(2)}, u32[]{:S(2)}) collective-permute-start(f32[4,32,256]{2,1,0:T(8,128)S(1)} %shard_map.74.refs_1_), channel_id=1, source_target_pairs={{0,8},{16,24},{32,40},{48,56},{64,72},{80,88},{96,104},{112,120},{... | collective-permute-start | bytes 393224 | tf_op jit(solution)/shard_map/ppermute | solution.py:157
  34.5 13.4 %collective-permute-start.6 = (f32[4,32,256]{2,1,0:T(8,128)S(1)}, f32[4,32,256]{2,1,0:T(8,128)S(1)}, u32[]{:S(2)}, u32[]{:S(2)}) collective-permute-start(f32[4,32,256]{2,1,0:T(8,128)S(1)} %shard_map.74.refs_1_), channel_id=1, source_target_pairs={{8,16},{24,32},{40,48},{56,64},{72,80},{88,96},{104,112},{120,128}... | collective-permute-start | bytes 393224 | tf_op jit(solution)/shard_map/ppermute | solution.py:157
  61.9 8.1 %collective-permute-start.9 = (f32[4,32,256]{2,1,0:T(8,128)S(1)}, f32[4,32,256]{2,1,0:T(8,128)S(1)}, u32[]{:S(2)}, u32[]{:S(2)}) collective-permute-start(f32[4,32,256]{2,1,0:T(8,128)S(1)} %get-tuple-element.31), channel_id=1, source_target_pairs={{8,16},{24,32},{40,48},{56,64},{72,80},{88,96},{104,112},{120,128}... | collective-permute-start | bytes 393224 | tf_op jit(solution)/shard_map/ppermute | solution.py:157
  67.1 6.9 %collective-permute-start.10 = (f32[4,32,256]{2,1,0:T(8,128)S(1)}, f32[4,32,256]{2,1,0:T(8,128)S(1)}, u32[]{:S(2)}, u32[]{:S(2)}) collective-permute-start(f32[4,32,256]{2,1,0:T(8,128)S(1)} %get-tuple-element.32), channel_id=1, source_target_pairs={{0,8},{16,24},{32,40},{48,56},{64,72},{80,88},{96,104},{112,120},{... | collective-permute-start | bytes 393224 | tf_op jit(solution)/shard_map/ppermute | solution.py:157

commit v6 on v4

--- a/solution.py
+++ b/solution.py
@@ -41,10 +41,11 @@
 
 def split_kernel(*refs):
     count = len(refs) // 3
-    for block, high, low in zip(refs[:count], refs[count::2], refs[count + 1 :: 2]):
+    for k, (block, high, low) in enumerate(zip(refs[:count], refs[count::2], refs[count + 1 :: 2])):
         for i in range(HB):
             rows = pl.ds(i * 256, 256)
-            high[rows, :], low[rows, :] = split(block[rows, :])
+            whole = block[rows, :]
+            high[rows, :], low[rows, :] = split(jnp.transpose(whole) if k < 2 else whole)
 
 
 def forward_kernel(line, parts, first, own, second, index_mine, index_theirs, *refs):
@@ -56,7 +57,8 @@
         total = None
         for s, (index, window) in enumerate(((index_mine, fields), (index_theirs, swapped(fields)))):
             high, low = (blocks[2 * s][rows, :], blocks[2 * s + 1][rows, :]) if parts else split(blocks[s][rows, :])
-            part = product(pick(window, index_tile(index, line + i)).reshape(n, 256), high, low, ((1,), (1,)))
+            picked = pick(window, index_tile(index, line + i)).reshape(n, 256)
+            part = product(picked, high, low, ((1,), (0,) if parts else (1,)))
             total = part if total is None else total + part
         for x in range(out.shape[0]):
             out[x, i] = total

time: 79.5 us -> 79.2 us (level)
  transfers between devices with their start and end apart: 8 -> 8, of which waited for: 4 -> 4; matrix products, arithmetic and copies ran while one was open for 0% -> 0% of each run, Pallas kernels for 3% -> 4%
where the time goes in v6:
time: 79.2 us; the launch traced here: 78.7 us
  starting transfers between devices  34.6 us (44%)
  blocking collectives  29.5 us (37%)
  waiting for transfers between devices  8.23 us (10%)
  Pallas kernels  6.3 us (8%)
    ppermute x6, starting transfers between devices, neighbours(): lax.ppermute(field, ('rows', 'core'), pairs + [(b, a) for a, b in pairs])  30.2 us
    all_to_all x2, blocking collectives, forward(): return lax.all_to_all(parts, 'x', 0, 0, tiled=True)  21 us
    all_to_all x1, blocking collectives, steps(): arrived = lax.all_to_all(packed, ('x', 'core'), 0, 0, tiled=True)  8.49 us
    ppermute x6, waiting for transfers between devices, neighbours(): lax.ppermute(field, ('rows', 'core'), pairs + [(b, a) for a, b in pairs])  8.23 us
    ppermute x1, starting transfers between devices, steps(): h_theirs = lax.ppermute(h, 'core', swap)  2.41 us
    pallas_call x1, Pallas kernels, steps(): call(split_kernel, (half,) * 8, 4, 1 << 20, 1 << 23)  2.19 us
    ppermute x1, starting transfers between devices, steps(): theirs = lax.ppermute(mine, 'core', swap)  1.92 us
  transfers between devices with their start and end apart: 8, of which 4 were waited for; matrix products, arithmetic and copies ran while one was open for 0% of the time, Pallas kernels for 4%

profile of v6, /device:TPU:16, one launch (start us, length us, event | category | flops | bytes accessed | tf_op | source)
XLA Modules:
  0.0 78.7 jit_solution(6450415808861469200)
XLA Ops:
  0.0 0.0 copy-start
  0.0 0.0 copy-start.1
  0.0 1.4 %stage.1.refs_3_.refs_5_.refs_2_.index_mine = f32[1032,256]{1,0:T(8,128)S(1)} custom-call(s32[4]{0:T(128)} %bitcast.9, s32[4]{0:T(128)} %refs_1_.1, s32[4]{0:T(128)} %bitcast.10, s32[4]{0:T(128)} %refs_3_.1, f32[1024,256]{1,0:T(8,128)} %bitcast.8), custom_call_target="tpu_custom_call" | custom-call | tf_op jit(solution)/shard_map/stage/pallas_call | solution.py:169
  1.4 1.9 %collective-permute-start.2 = (f32[1032,256]{1,0:T(8,128)S(1)}, f32[1032,256]{1,0:T(8,128)S(1)}, u32[]{:S(2)}, u32[]{:S(2)}) collective-permute-start(f32[1032,256]{1,0:T(8,128)S(1)} %stage.1.refs_3_.refs_5_.refs_2_.index_mine), channel_id=1, source_target_pairs={{0,1},{1,0},{2,3},{3,2},{4,5},{5,4},{6,7},{7,6},{8,9},{9,8},{10,11... | collective-permute-start | bytes 3170312 | tf_op jit(solution)/shard_map/ppermute | solution.py:183
  3.3 0.0 copy-done.1
  3.3 2.4 %collective-permute-start.5 = (f32[1024,256]{1,0:T(8,128)S(1)}, f32[1024,256]{1,0:T(8,128)}, u32[]{:S(2)}, u32[]{:S(2)}) collective-permute-start(f32[1024,256]{1,0:T(8,128)S(1)} %bitcast.6), channel_id=1, source_target_pairs={{0,1},{1,0},{2,3},{3,2},{4,5},{5,4},{6,7},{7,6},{8,9},{9,8},{10,11... | collective-permute-start | bytes 3145736 | tf_op jit(solution)/shard_map/ppermute | solution.py:184
  5.7 0.0 copy-done
  5.8 3.5 %collective-permute-start.1 = (f32[4,32,256]{2,1,0:T(8,128)S(1)}, f32[4,32,256]{2,1,0:T(8,128)S(1)}, u32[]{:S(2)}, u32[]{:S(2)}) collective-permute-start(f32[4,32,256]{2,1,0:T(8,128)S(1)} %dynamic-slice_bitcast_fusion.refs_1_), channel_id=1, source_target_pairs={{0,8},{16,24},{32,40},{48,56},{64,72},{80,88},{96,104},{112,120},{... | collective-permute-start | bytes 393224 | tf_op jit(solution)/shard_map/ppermute | solution.py:159
  9.3 13.9 %collective-permute-start = (f32[4,32,256]{2,1,0:T(8,128)S(1)}, f32[4,32,256]{2,1,0:T(8,128)S(1)}, u32[]{:S(2)}, u32[]{:S(2)}) collective-permute-start(f32[4,32,256]{2,1,0:T(8,128)S(1)} %dynamic-slice_bitcast_fusion.refs_1_), channel_id=1, source_target_pairs={{8,16},{24,32},{40,48},{56,64},{72,80},{88,96},{104,112},{120,128}... | collective-permute-start | bytes 393224 | tf_op jit(solution)/shard_map/ppermute | solution.py:159
  23.1 0.0 collective-permute-done.1.refs_2_
  23.1 2.9 %collective-permute-done.refs_0_ = f32[4,32,256]{2,1,0:T(8,128)S(1)} collective-permute-done((f32[4,32,256]{2,1,0:T(8,128)S(1)}, f32[4,32,256]{2,1,0:T(8,128)S(1)}, u32[]{:S(2)}, u32[]{:S(2)}) %collective-permute-start) | collective-permute-done | bytes 131104 | tf_op jit(solution)/shard_map/ppermute | solution.py:159
  26.1 0.0 collective-permute-done.2.refs_4_.refs_6_.refs_3_.index_theirs
  26.1 0.8 %shard_map.73 = f32[4,4,32,256]{3,2,1,0:T(8,128)S(1)} custom-call(f32[4,32,256]{2,1,0:T(8,128)S(1)} %collective-permute-done.refs_0_, f32[4,32,256]{2,1,0:T(8,128)S(1)} %dynamic-slice_bitcast_fusion.refs_1_, f32[4,32,256]{2,1,0:T(8,128)S(1)} %collective-permute-done.1.refs_2_, f32[1032,256]{1,0:T(8,128)S(1)} %stage.1.refs_3_.refs_5_.refs_2_.index_mine, ...), custom_call_target="tpu_custom_call" | custom-call | flops 268435456 | bytes 4194304 | tf_op jit(solution)/shard_map/pallas_call | solution.py:189
  26.9 10.5 %all_to_all.15.parts = f32[4,4,32,256]{3,2,1,0:T(8,128)S(1)} all-to-all(f32[4,4,32,256]{3,2,1,0:T(8,128)S(1)} %shard_map.73), channel_id=1, replica_groups=mesh['rows'=128,'x'=4,'core'=2] {'x'}, dimensions={0} | all-to-all | bytes 1048576 | tf_op jit(solution)/shard_map/all_to_all | solution.py:190
  37.4 1.9 %collective-permute-start.4 = (f32[4,32,256]{2,1,0:T(8,128)S(1)}, f32[4,32,256]{2,1,0:T(8,128)S(1)}, u32[]{:S(2)}, u32[]{:S(2)}) collective-permute-start(f32[4,32,256]{2,1,0:T(8,128)S(1)} %shard_map.74.refs_1_), channel_id=1, source_target_pairs={{0,8},{16,24},{32,40},{48,56},{64,72},{80,88},{96,104},{112,120},{... | collective-permute-start | bytes 393224 | tf_op jit(solution)/shard_map/ppermute | solution.py:159
  39.3 4.8 %collective-permute-start.3 = (f32[4,32,256]{2,1,0:T(8,128)S(1)}, f32[4,32,256]{2,1,0:T(8,128)S(1)}, u32[]{:S(2)}, u32[]{:S(2)}) collective-permute-start(f32[4,32,256]{2,1,0:T(8,128)S(1)} %shard_map.74.refs_1_), channel_id=1, source_target_pairs={{8,16},{24,32},{40,48},{56,64},{72,80},{88,96},{104,112},{120,128}... | collective-permute-start | bytes 393224 | tf_op jit(solution)/shard_map/ppermute | solution.py:159
  44.1 0.0 collective-permute-done.5.refs_1_
  44.1 2.2 %shard_map.75 = (bf16[1024,256]{1,0:T(8,128)(2,1)S(1)}, bf16[1024,256]{1,0:T(8,128)(2,1)S(1)}, bf16[1024,256]{1,0:T(8,128)(2,1)S(1)}, bf16[1024,256]{1,0:T(8,128...) custom-call(f32[1024,256]{1,0:T(8,128)S(1)} %bitcast.7, ...), custom_call_target="tpu_custom_call" | custom-call | flops 1048576 | bytes 8388608 | tf_op jit(solution)/shard_map/pallas_call | solution.py:196
  46.3 0.0 collective-permute-done.4.refs_2_
  46.3 0.7 collective-permute-done.3.refs_0_
  47.0 0.4 shard_map.76
  47.5 10.5 %all_to_all.16.parts = f32[4,4,32,256]{3,2,1,0:T(8,128)S(1)} all-to-all(f32[4,4,32,256]{3,2,1,0:T(8,128)S(1)} %shard_map.76), channel_id=1, replica_groups=mesh['rows'=128,'x'=4,'core'=2] {'x'}, dimensions={0} | all-to-all | bytes 1048576 | tf_op jit(solution)/shard_map/all_to_all | solution.py:190
  58.0 0.6 shard_map.77
  58.5 3.9 %collective-permute-start.6 = (f32[4,32,256]{2,1,0:T(8,128)S(1)}, f32[4,32,256]{2,1,0:T(8,128)S(1)}, u32[]{:S(2)}, u32[]{:S(2)}) collective-permute-start(f32[4,32,256]{2,1,0:T(8,128)S(1)} %get-tuple-element.31), channel_id=1, source_target_pairs={{8,16},{24,32},{40,48},{56,64},{72,80},{88,96},{104,112},{120,128}... | collective-permute-start | bytes 393224 | tf_op jit(solution)/shard_map/ppermute | solution.py:159
  62.5 2.3 %collective-permute-start.7 = (f32[4,32,256]{2,1,0:T(8,128)S(1)}, f32[4,32,256]{2,1,0:T(8,128)S(1)}, u32[]{:S(2)}, u32[]{:S(2)}) collective-permute-start(f32[4,32,256]{2,1,0:T(8,128)S(1)} %get-tuple-element.32), channel_id=1, source_target_pairs={{0,8},{16,24},{32,40},{48,56},{64,72},{80,88},{96,104},{112,120},{... | collective-permute-start | bytes 393224 | tf_op jit(solution)/shard_map/ppermute | solution.py:159
  64.7 0.7 collective-permute-done.6.below
  65.4 3.9 %collective-permute-done.7.above = f32[4,32,256]{2,1,0:T(8,128)S(1)} collective-permute-done((f32[4,32,256]{2,1,0:T(8,128)S(1)}, f32[4,32,256]{2,1,0:T(8,128)S(1)}, u32[]{:S(2)}, u32[]{:S(2)}) %collective-permute-start.7) | collective-permute-done | bytes 131104 | tf_op jit(solution)/shard_map/ppermute | solution.py:159
  69.3 0.2 shard_map.78
  69.5 8.5 %all_to_all.17.parts = f32[8,32,128]{2,1,0:T(8,128)S(1)} all-to-all(f32[8,32,128]{2,1,0:T(8,128)S(1)} %shard_map.78), channel_id=1, replica_groups=mesh['rows'=128,'x'=4,'core'=2] {'x','core'}, dimensions={0} | all-to-all | bytes 262144 | tf_op jit(solution)/shard_map/all_to_all | solution.py:204
  78.0 0.7 shard_map.79
  (2 shorter events, 0.0 us)
Async XLA Ops:
  0.0 5.7 %copy-start = (f32[4,256,64]{1,2,0:T(8,128)S(1)}, f32[4,256,64]{1,2,0:T(8,128)}, u32[]{:S(2)}) copy-start(f32[4,256,64]{1,2,0:T(8,128)} %param.13) | copy-start | bytes 786436
  0.0 3.3 %copy-start.1 = (f32[4,1,256,256]{3,2,1,0:T(8,128)S(1)}, f32[4,1,256,256]{3,2,1,0:T(8,128)}, u32[]{:S(2)}) copy-start(f32[4,1,256,256]{3,2,1,0:T(8,128)} %param.10) | copy-start | bytes 3145732
  1.4 24.7 %collective-permute-start.2 = (f32[1032,256]{1,0:T(8,128)S(1)}, f32[1032,256]{1,0:T(8,128)S(1)}, u32[]{:S(2)}, u32[]{:S(2)}) collective-permute-start(f32[1032,256]{1,0:T(8,128)S(1)} %stage.1.refs_3_.refs_5_.refs_2_.index_mine), channel_id=1, source_target_pairs={{0,1},{1,0},{2,3},{3,2},{4,5},{5,4},{6,7},{7,6},{8,9},{9,8},{10,11... | collective-permute-start | bytes 3170312 | tf_op jit(solution)/shard_map/ppermute | solution.py:183
  3.3 40.8 %collective-permute-start.5 = (f32[1024,256]{1,0:T(8,128)S(1)}, f32[1024,256]{1,0:T(8,128)}, u32[]{:S(2)}, u32[]{:S(2)}) collective-permute-start(f32[1024,256]{1,0:T(8,128)S(1)} %bitcast.6), channel_id=1, source_target_pairs={{0,1},{1,0},{2,3},{3,2},{4,5},{5,4},{6,7},{7,6},{8,9},{9,8},{10,11... | collective-permute-start | bytes 3145736 | tf_op jit(solution)/shard_map/ppermute | solution.py:184
  5.8 17.4 %collective-permute-start.1 = (f32[4,32,256]{2,1,0:T(8,128)S(1)}, f32[4,32,256]{2,1,0:T(8,128)S(1)}, u32[]{:S(2)}, u32[]{:S(2)}) collective-permute-start(f32[4,32,256]{2,1,0:T(8,128)S(1)} %dynamic-slice_bitcast_fusion.refs_1_), channel_id=1, source_target_pairs={{0,8},{16,24},{32,40},{48,56},{64,72},{80,88},{96,104},{112,120},{... | collective-permute-start | bytes 393224 | tf_op jit(solution)/shard_map/ppermute | solution.py:159
  9.3 16.8 %collective-permute-start = (f32[4,32,256]{2,1,0:T(8,128)S(1)}, f32[4,32,256]{2,1,0:T(8,128)S(1)}, u32[]{:S(2)}, u32[]{:S(2)}) collective-permute-start(f32[4,32,256]{2,1,0:T(8,128)S(1)} %dynamic-slice_bitcast_fusion.refs_1_), channel_id=1, source_target_pairs={{8,16},{24,32},{40,48},{56,64},{72,80},{88,96},{104,112},{120,128}... | collective-permute-start | bytes 393224 | tf_op jit(solution)/shard_map/ppermute | solution.py:159
  37.4 8.9 %collective-permute-start.4 = (f32[4,32,256]{2,1,0:T(8,128)S(1)}, f32[4,32,256]{2,1,0:T(8,128)S(1)}, u32[]{:S(2)}, u32[]{:S(2)}) collective-permute-start(f32[4,32,256]{2,1,0:T(8,128)S(1)} %shard_map.74.refs_1_), channel_id=1, source_target_pairs={{0,8},{16,24},{32,40},{48,56},{64,72},{80,88},{96,104},{112,120},{... | collective-permute-start | bytes 393224 | tf_op jit(solution)/shard_map/ppermute | solution.py:159
  39.3 7.7 %collective-permute-start.3 = (f32[4,32,256]{2,1,0:T(8,128)S(1)}, f32[4,32,256]{2,1,0:T(8,128)S(1)}, u32[]{:S(2)}, u32[]{:S(2)}) collective-permute-start(f32[4,32,256]{2,1,0:T(8,128)S(1)} %shard_map.74.refs_1_), channel_id=1, source_target_pairs={{8,16},{24,32},{40,48},{56,64},{72,80},{88,96},{104,112},{120,128}... | collective-permute-start | bytes 393224 | tf_op jit(solution)/shard_map/ppermute | solution.py:159
  58.5 6.9 %collective-permute-start.6 = (f32[4,32,256]{2,1,0:T(8,128)S(1)}, f32[4,32,256]{2,1,0:T(8,128)S(1)}, u32[]{:S(2)}, u32[]{:S(2)}) collective-permute-start(f32[4,32,256]{2,1,0:T(8,128)S(1)} %get-tuple-element.31), channel_id=1, source_target_pairs={{8,16},{24,32},{40,48},{56,64},{72,80},{88,96},{104,112},{120,128}... | collective-permute-start | bytes 393224 | tf_op jit(solution)/shard_map/ppermute | solution.py:159
  62.5 6.9 %collective-permute-start.7 = (f32[4,32,256]{2,1,0:T(8,128)S(1)}, f32[4,32,256]{2,1,0:T(8,128)S(1)}, u32[]{:S(2)}, u32[]{:S(2)}) collective-permute-start(f32[4,32,256]{2,1,0:T(8,128)S(1)} %get-tuple-element.32), channel_id=1, source_target_pairs={{0,8},{16,24},{32,40},{48,56},{64,72},{80,88},{96,104},{112,120},{... | collective-permute-start | bytes 393224 | tf_op jit(solution)/shard_map/ppermute | solution.py:159
